TPU v7x, 256 devices: a whole 4x4x8 slice. The times are simulated.
256 devices in a mesh: dp: 16 (over y_hi, x, core), seq: 16 (over y_lo, z).
Axes of the slice: x: 4, y: 4 (y_hi: 2, y_lo: 2; y = y_hi * 2 + y_lo), z: 8, core: 2. Of those that a mesh axis runs over, the one named last changes fastest.
Arguments:
- queries: bfloat16 [32768, 1280], P(('dp', 'seq')), may hold values from -6 to 6
- key_states: bfloat16 [32768, 1280], P(('dp', 'seq')), may hold values from -6 to 6
- value_states: bfloat16 [32768, 1280], P(('dp', 'seq')), may hold values from -6 to 6
- out_grads: bfloat16 [32768, 1280], P(('dp', 'seq')), may hold values from -6 to 6
- row_order: int32 [32768], P(('dp', 'seq')), may hold values from 0 to 127, as said below
- segment_ids: int32 [16, 2048], P('dp'), may hold values from 0 to 1, as said below
Outputs:
- grad_queries: bfloat16 [32768, 1280], P(('dp', 'seq'))
- grad_keys: bfloat16 [32768, 1280], P(('dp', 'seq'))
- grad_values: bfloat16 [32768, 1280], P(('dp', 'seq'))
Inputs may be any that keep to these rules, and one draw needn't show every extreme that they name: `row_order`: each block of 128 entries names every number of 0 to 127 once. `segment_ids`: each row holds two screenshots: ids 0 then 1, never falling; the first row with id 1 lies between 768 and 1280.
All inputs are finite; a program needn't handle non-finite values.
Results may differ from a plain program's by a relative error of at most 0.012.
Values may be sent and summed in bfloat16 or wider, within the bound.
A program may use at most 64 MiB of HBM per device.

v0:
```python
import math

import jax
import jax.numpy as jnp
from jax import lax
from jax.sharding import PartitionSpec as P

HD = 80


NEG_FILL = -1e30


def block_count(length):
    return max(1, length // 512)


def score_block(query_block, key_block, query_seg, key_seg, inv_root):
    scores = (
        jnp.einsum("qhd,khd->hqk", query_block, key_block, preferred_element_type=jnp.float32)
        * inv_root
    )
    matched = query_seg[:, None] == key_seg[None, :]
    return jnp.where(matched[None], scores, NEG_FILL)


def row_delta(grad_block, attended):
    return jnp.sum(grad_block.astype(jnp.float32) * attended, axis=-1).T[:, :, None]


def dense_grads(query_rows, key_rows, value_rows, grad_rows, query_seg, key_seg, inv_root):
    rows = query_rows.shape[0]
    blocks = block_count(rows)
    span = rows // blocks

    def visit(block_index, carry):
        grad_q, grad_k, grad_v = carry
        start = block_index * span
        query_block = lax.dynamic_slice_in_dim(query_rows, start, span, 0)
        grad_block = lax.dynamic_slice_in_dim(grad_rows, start, span, 0)
        seg_block = lax.dynamic_slice_in_dim(query_seg, start, span, 0)
        scores = score_block(query_block, key_rows, seg_block, key_seg, inv_root)
        shifted = jnp.exp(scores - jnp.max(scores, axis=-1, keepdims=True))
        probs = shifted / jnp.sum(shifted, axis=-1, keepdims=True)
        probs_low = probs.astype(jnp.bfloat16)
        attended = jnp.einsum(
            "hqk,khd->qhd", probs_low, value_rows, preferred_element_type=jnp.float32
        )
        delta = row_delta(grad_block, attended)
        dprobs = jnp.einsum(
            "qhd,khd->hqk", grad_block, value_rows, preferred_element_type=jnp.float32
        )
        dscores = (probs * (dprobs - delta) * inv_root).astype(jnp.bfloat16)
        block_grad = jnp.einsum(
            "hqk,khd->qhd", dscores, key_rows, preferred_element_type=jnp.float32
        ).astype(jnp.bfloat16)
        grad_k = grad_k + jnp.einsum(
            "hqk,qhd->khd", dscores, query_block, preferred_element_type=jnp.float32
        )
        grad_v = grad_v + jnp.einsum(
            "hqk,qhd->khd", probs_low, grad_block, preferred_element_type=jnp.float32
        )
        grad_q = lax.dynamic_update_slice_in_dim(grad_q, block_grad, start, 0)
        return (grad_q, grad_k, grad_v)

    start_state = (
        jnp.zeros(query_rows.shape, jnp.bfloat16),
        jnp.zeros(key_rows.shape, jnp.float32),
        jnp.zeros(key_rows.shape, jnp.float32),
    )
    return lax.fori_loop(0, blocks, visit, start_state)


def on_device(queries, key_states, value_states, out_grads, row_order, segment_ids):
    rows = queries.shape[0]
    heads = queries.shape[1] // HD
    inv_root = 1.0 / math.sqrt(HD)
    group_seg = segment_ids[0]
    permuted = (
        queries[row_order],
        key_states[row_order],
        value_states[row_order],
        out_grads[row_order],
    )
    moved = (
        lax.all_to_all(permuted[0], "dp", split_axis=0, concat_axis=0, tiled=True),
        lax.all_to_all(permuted[1], "dp", split_axis=0, concat_axis=0, tiled=True),
        lax.all_to_all(permuted[2], "dp", split_axis=0, concat_axis=0, tiled=True),
        lax.all_to_all(permuted[3], "dp", split_axis=0, concat_axis=0, tiled=True),
    )
    shaped = tuple((item.reshape(rows, heads, HD) for item in moved))
    seq_devs = lax.axis_size("seq")
    own_heads = heads // seq_devs
    split_form = tuple((item.reshape(rows, seq_devs, own_heads, HD) for item in shaped))
    parts = (
        lax.all_to_all(split_form[0], "seq", split_axis=1, concat_axis=0, tiled=True),
        lax.all_to_all(split_form[1], "seq", split_axis=1, concat_axis=0, tiled=True),
        lax.all_to_all(split_form[2], "seq", split_axis=1, concat_axis=0, tiled=True),
        lax.all_to_all(split_form[3], "seq", split_axis=1, concat_axis=0, tiled=True),
    )
    flat_parts = tuple((part[:, 0] for part in parts))
    grads = dense_grads(
        flat_parts[0], flat_parts[1], flat_parts[2], flat_parts[3], group_seg, group_seg, inv_root
    )
    grad_q, grad_k, grad_v = (
        lax.all_to_all(grads[0][:, None], "seq", split_axis=0, concat_axis=1, tiled=True),
        lax.all_to_all(
            grads[1].astype(jnp.bfloat16)[:, None], "seq", split_axis=0, concat_axis=1, tiled=True
        ),
        lax.all_to_all(
            grads[2].astype(jnp.bfloat16)[:, None], "seq", split_axis=0, concat_axis=1, tiled=True
        ),
    )
    flat = (
        grad_q.reshape(rows, heads * HD),
        grad_k.reshape(rows, heads * HD),
        grad_v.reshape(rows, heads * HD),
    )
    returned = (
        lax.all_to_all(flat[0], "dp", split_axis=0, concat_axis=0, tiled=True),
        lax.all_to_all(flat[1], "dp", split_axis=0, concat_axis=0, tiled=True),
        lax.all_to_all(flat[2], "dp", split_axis=0, concat_axis=0, tiled=True),
    )
    positions = jnp.arange(rows, dtype=jnp.int32)
    inverse = jnp.zeros_like(row_order).at[row_order].set(positions)
    return (returned[0][inverse], returned[1][inverse], returned[2][inverse])


def solution(mesh):
    placed = (
        P(("dp", "seq"), None),
        P(("dp", "seq"), None),
        P(("dp", "seq"), None),
        P(("dp", "seq"), None),
        P(("dp", "seq")),
        P("dp", None),
    )
    return jax.shard_map(
        on_device,
        mesh=mesh,
        in_specs=placed,
        out_specs=(P(("dp", "seq"), None), P(("dp", "seq"), None), P(("dp", "seq"), None)),
        check_vma=False,
    )
```

profile of v0, /device:TPU:1, one launch (start us, length us, event | category | flops | bytes accessed | tf_op | source)
XLA Modules:
  0.0 277.4 jit_solution(156224822939703460)
XLA Ops:
  3.2 8.6 %all-to-all-start = ((bf16[16,8,1280]{2,1,0:T(8,128)(2,1)}), bf16[16,8,1280]{2,1,0:T(8,128)(2,1)S(1)}, u32[]{:S(2)}, u32[]{:S(2)}) async-start(bf16[16,8,1280]{2,1,0:T(8,128)(2,1)} %bitcast.1), calls=%async_computation | async-start | bytes 655360 | tf_op jit(solution)/shard_map/all_to_all | solution.py:86
  13.4 7.6 %all-to-all-done = bf16[16,8,1280]{2,1,0:T(8,128)(2,1)S(1)} async-done(((bf16[16,8,1280]{2,1,0:T(8,128)(2,1)}), bf16[16,8,1280]{2,1,0:T(8,128)(2,1)S(1)}, u32[]{:S(2)}, u32[]{:S(2)}) %all-to-all-start) | async-done | bytes 327712 | tf_op jit(solution)/shard_map/all_to_all | solution.py:86
  21.0 4.3 %all-to-all-start.2 = ((bf16[16,8,1280]{2,1,0:T(8,128)(2,1)}), bf16[16,8,1280]{2,1,0:T(8,128)(2,1)S(1)}, u32[]{:S(2)}, u32[]{:S(2)}) async-start(bf16[16,8,1280]{2,1,0:T(8,128)(2,1)} %bitcast.4), calls=%async_computation.2 | async-start | bytes 655360 | tf_op jit(solution)/shard_map/all_to_all | solution.py:87
  26.8 7.6 %all-to-all-done.2 = bf16[16,8,1280]{2,1,0:T(8,128)(2,1)S(1)} async-done(((bf16[16,8,1280]{2,1,0:T(8,128)(2,1)}), bf16[16,8,1280]{2,1,0:T(8,128)(2,1)S(1)}, u32[]{:S(2)}, u32[]{:S(2)}) %all-to-all-start.2) | async-done | bytes 327712 | tf_op jit(solution)/shard_map/all_to_all | solution.py:87
  34.5 4.3 %all-to-all-start.4 = ((bf16[16,8,1280]{2,1,0:T(8,128)(2,1)}), bf16[16,8,1280]{2,1,0:T(8,128)(2,1)S(1)}, u32[]{:S(2)}, u32[]{:S(2)}) async-start(bf16[16,8,1280]{2,1,0:T(8,128)(2,1)} %bitcast.7), calls=%async_computation.4 | async-start | bytes 655360 | tf_op jit(solution)/shard_map/all_to_all | solution.py:89
  40.4 7.6 %all-to-all-done.4 = bf16[16,8,1280]{2,1,0:T(8,128)(2,1)S(1)} async-done(((bf16[16,8,1280]{2,1,0:T(8,128)(2,1)}), bf16[16,8,1280]{2,1,0:T(8,128)(2,1)S(1)}, u32[]{:S(2)}, u32[]{:S(2)}) %all-to-all-start.4) | async-done | bytes 327712 | tf_op jit(solution)/shard_map/all_to_all | solution.py:89
  48.0 4.3 %all-to-all-start.6 = ((bf16[16,8,1280]{2,1,0:T(8,128)(2,1)}), bf16[16,8,1280]{2,1,0:T(8,128)(2,1)S(1)}, u32[]{:S(2)}, u32[]{:S(2)}) async-start(bf16[16,8,1280]{2,1,0:T(8,128)(2,1)} %bitcast.10), calls=%async_computation.6 | async-start | bytes 655360 | tf_op jit(solution)/shard_map/all_to_all | solution.py:88
  54.2 7.3 %all-to-all-done.6 = bf16[16,8,1280]{2,1,0:T(8,128)(2,1)S(1)} async-done(((bf16[16,8,1280]{2,1,0:T(8,128)(2,1)}), bf16[16,8,1280]{2,1,0:T(8,128)(2,1)S(1)}, u32[]{:S(2)}, u32[]{:S(2)}) %all-to-all-start.6) | async-done | bytes 327712 | tf_op jit(solution)/shard_map/all_to_all | solution.py:88
  61.5 8.4 %all-to-all-start.1 = ((bf16[128,16,1,80]{0,3,2,1:T(8,128)(2,1)}), bf16[128,16,1,80]{0,3,2,1:T(8,128)(2,1)S(1)}, u32[]{:S(2)}, u32[]{:S(2)}) async-start(bf16[128,16,1,80]{0,3,2,1:T(8,128)(2,1)} %copy.43), calls=%async_computation.1 | async-start | bytes 655360 | tf_op jit(solution)/shard_map/all_to_all | solution.py:96
  71.9 7.7 %all-to-all-done.1 = bf16[128,16,1,80]{0,3,2,1:T(8,128)(2,1)S(1)} async-done(((bf16[128,16,1,80]{0,3,2,1:T(8,128)(2,1)}), bf16[128,16,1,80]{0,3,2,1:T(8,128)(2,1)S(1)}, u32[]{:S(2)}, u32[]{:S(2)}) %all-to-all-start.1) | async-done | bytes 327712 | tf_op jit(solution)/shard_map/all_to_all | solution.py:96
  79.6 5.9 %all-to-all-start.3 = ((bf16[128,16,1,80]{0,3,2,1:T(8,128)(2,1)}), bf16[128,16,1,80]{0,3,2,1:T(8,128)(2,1)S(1)}, u32[]{:S(2)}, u32[]{:S(2)}) async-start(bf16[128,16,1,80]{0,3,2,1:T(8,128)(2,1)} %copy.45), calls=%async_computation.3 | async-start | bytes 655360 | tf_op jit(solution)/shard_map/all_to_all | solution.py:97
  87.5 7.4 %all-to-all-done.3 = bf16[128,16,1,80]{0,3,2,1:T(8,128)(2,1)S(1)} async-done(((bf16[128,16,1,80]{0,3,2,1:T(8,128)(2,1)}), bf16[128,16,1,80]{0,3,2,1:T(8,128)(2,1)S(1)}, u32[]{:S(2)}, u32[]{:S(2)}) %all-to-all-start.3) | async-done | bytes 327712 | tf_op jit(solution)/shard_map/all_to_all | solution.py:97
  94.9 6.1 %all-to-all-start.5 = ((bf16[128,16,1,80]{0,3,2,1:T(8,128)(2,1)}), bf16[128,16,1,80]{0,3,2,1:T(8,128)(2,1)S(1)}, u32[]{:S(2)}, u32[]{:S(2)}) async-start(bf16[128,16,1,80]{0,3,2,1:T(8,128)(2,1)} %copy.47), calls=%async_computation.5 | async-start | bytes 655360 | tf_op jit(solution)/shard_map/all_to_all | solution.py:99
  102.9 7.1 %all-to-all-done.5 = bf16[128,16,1,80]{0,3,2,1:T(8,128)(2,1)S(1)} async-done(((bf16[128,16,1,80]{0,3,2,1:T(8,128)(2,1)}), bf16[128,16,1,80]{0,3,2,1:T(8,128)(2,1)S(1)}, u32[]{:S(2)}, u32[]{:S(2)}) %all-to-all-start.5) | async-done | bytes 327712 | tf_op jit(solution)/shard_map/all_to_all | solution.py:99
  110.0 6.4 %all-to-all-start.7 = ((bf16[128,16,1,80]{0,3,2,1:T(8,128)(2,1)}), bf16[128,16,1,80]{0,3,2,1:T(8,128)(2,1)S(1)}, u32[]{:S(2)}, u32[]{:S(2)}) async-start(bf16[128,16,1,80]{0,3,2,1:T(8,128)(2,1)} %copy.49), calls=%async_computation.7 | async-start | bytes 655360 | tf_op jit(solution)/shard_map/all_to_all | solution.py:98
  119.3 6.1 %all-to-all-done.7 = bf16[128,16,1,80]{0,3,2,1:T(8,128)(2,1)S(1)} async-done(((bf16[128,16,1,80]{0,3,2,1:T(8,128)(2,1)}), bf16[128,16,1,80]{0,3,2,1:T(8,128)(2,1)S(1)}, u32[]{:S(2)}, u32[]{:S(2)}) %all-to-all-start.7) | async-done | bytes 327712 | tf_op jit(solution)/shard_map/all_to_all | solution.py:98
  126.4 54.6 %while.18 = (s32[]{:T(128)}, bf16[2048,1,80]{0,2,1:T(8,128)(2,1)}, f32[2048,1,80]{0,2,1:T(8,128)}, f32[2048,1,80]{0,2,1:T(8,128)S(1)}, s32[2048]{0:T(1024)S(1)},...) while((s32[]{:T(128)}, bf16[2048,1,80]{0,2,1:T(8,128)(2,1)}, ...), condition=%wide.region_4.5_spmd.clone, body=%wide.region_0.4_spmd.clone.sunk | while | flops 1022130688 | bytes 73658640 | solution.py:71
  147.1 2.6 fusion.63
  160.8 2.6 fusion.63
  174.5 2.6 fusion.63
  185.7 6.4 %all-to-all-start.12 = ((bf16[16,2,5120]{2,1,0:T(2,128)(2,1)}), bf16[16,2,5120]{2,1,0:T(2,128)(2,1)S(1)}, u32[]{:S(2)}, u32[]{:S(2)}) async-start(bf16[16,2,5120]{2,1,0:T(2,128)(2,1)} %reshape.200), calls=%async_computation.12 | async-start | bytes 655360 | tf_op jit(solution)/shard_map/all_to_all | solution.py:110
  195.0 6.1 %all-to-all-done.12 = bf16[16,2,5120]{2,1,0:T(2,128)(2,1)S(1)} async-done(((bf16[16,2,5120]{2,1,0:T(2,128)(2,1)}), bf16[16,2,5120]{2,1,0:T(2,128)(2,1)S(1)}, u32[]{:S(2)}, u32[]{:S(2)}) %all-to-all-start.12) | async-done | bytes 327712 | tf_op jit(solution)/shard_map/all_to_all | solution.py:110
  201.1 6.4 %all-to-all-start.10 = ((bf16[16,2,5120]{2,1,0:T(2,128)(2,1)}), bf16[16,2,5120]{2,1,0:T(2,128)(2,1)S(1)}, u32[]{:S(2)}, u32[]{:S(2)}) async-start(bf16[16,2,5120]{2,1,0:T(2,128)(2,1)} %reshape.198), calls=%async_computation.10 | async-start | bytes 655360 | tf_op jit(solution)/shard_map/all_to_all | solution.py:107
  210.4 6.1 %all-to-all-done.10 = bf16[16,2,5120]{2,1,0:T(2,128)(2,1)S(1)} async-done(((bf16[16,2,5120]{2,1,0:T(2,128)(2,1)}), bf16[16,2,5120]{2,1,0:T(2,128)(2,1)S(1)}, u32[]{:S(2)}, u32[]{:S(2)}) %all-to-all-start.10) | async-done | bytes 327712 | tf_op jit(solution)/shard_map/all_to_all | solution.py:107
  216.6 6.4 %all-to-all-start.8 = ((bf16[16,2,5120]{2,1,0:T(2,128)(2,1)}), bf16[16,2,5120]{2,1,0:T(2,128)(2,1)S(1)}, u32[]{:S(2)}, u32[]{:S(2)}) async-start(bf16[16,2,5120]{2,1,0:T(2,128)(2,1)} %reshape.196), calls=%async_computation.8 | async-start | bytes 655360 | tf_op jit(solution)/shard_map/all_to_all | solution.py:106
  226.7 5.3 %all-to-all-done.8 = bf16[16,2,5120]{2,1,0:T(2,128)(2,1)S(1)} async-done(((bf16[16,2,5120]{2,1,0:T(2,128)(2,1)}), bf16[16,2,5120]{2,1,0:T(2,128)(2,1)S(1)}, u32[]{:S(2)}, u32[]{:S(2)}) %all-to-all-start.8) | async-done | bytes 327712 | tf_op jit(solution)/shard_map/all_to_all | solution.py:106
  232.0 7.6 %all-to-all-start.13 = ((bf16[16,8,1280]{2,1,0:T(8,128)(2,1)}), bf16[16,8,1280]{2,1,0:T(8,128)(2,1)S(1)}, u32[]{:S(2)}, u32[]{:S(2)}) async-start(bf16[16,8,1280]{2,1,0:T(8,128)(2,1)} %all_to_all.160), calls=%async_computation.13 | async-start | bytes 655360 | tf_op jit(solution)/shard_map/all_to_all | solution.py:122
  243.3 5.5 %all-to-all-done.13 = bf16[16,8,1280]{2,1,0:T(8,128)(2,1)S(1)} async-done(((bf16[16,8,1280]{2,1,0:T(8,128)(2,1)}), bf16[16,8,1280]{2,1,0:T(8,128)(2,1)S(1)}, u32[]{:S(2)}, u32[]{:S(2)}) %all-to-all-start.13) | async-done | bytes 327712 | tf_op jit(solution)/shard_map/all_to_all | solution.py:122
  248.8 4.3 %all-to-all-start.11 = ((bf16[16,8,1280]{2,1,0:T(8,128)(2,1)}), bf16[16,8,1280]{2,1,0:T(8,128)(2,1)S(1)}, u32[]{:S(2)}, u32[]{:S(2)}) async-start(bf16[16,8,1280]{2,1,0:T(8,128)(2,1)} %all_to_all.154), calls=%async_computation.11 | async-start | bytes 655360 | tf_op jit(solution)/shard_map/all_to_all | solution.py:121
  257.7 4.6 %all-to-all-done.11 = bf16[16,8,1280]{2,1,0:T(8,128)(2,1)S(1)} async-done(((bf16[16,8,1280]{2,1,0:T(8,128)(2,1)}), bf16[16,8,1280]{2,1,0:T(8,128)(2,1)S(1)}, u32[]{:S(2)}, u32[]{:S(2)}) %all-to-all-start.11) | async-done | bytes 327712 | tf_op jit(solution)/shard_map/all_to_all | solution.py:121
  262.3 4.3 %all-to-all-start.9 = ((bf16[16,8,1280]{2,1,0:T(8,128)(2,1)}), bf16[16,8,1280]{2,1,0:T(8,128)(2,1)S(1)}, u32[]{:S(2)}, u32[]{:S(2)}) async-start(bf16[16,8,1280]{2,1,0:T(8,128)(2,1)} %all_to_all.148), calls=%async_computation.9 | async-start | bytes 655360 | tf_op jit(solution)/shard_map/all_to_all | solution.py:120
  269.8 6.0 %all-to-all-done.9 = bf16[16,8,1280]{2,1,0:T(8,128)(2,1)S(1)} async-done(((bf16[16,8,1280]{2,1,0:T(8,128)(2,1)}), bf16[16,8,1280]{2,1,0:T(8,128)(2,1)S(1)}, u32[]{:S(2)}, u32[]{:S(2)}) %all-to-all-start.9) | async-done | bytes 327712 | tf_op jit(solution)/shard_map/all_to_all | solution.py:120
  (119 shorter events, 92.8 us)
Async XLA Ops:
  0.6 1.0 copy-start
  0.6 11.1 %copy-start.3 = (bf16[128,1280]{1,0:T(8,128)(2,1)S(1)}, bf16[128,1280]{1,0:T(8,128)(2,1)}, u32[]{:S(2)}) copy-start(bf16[128,1280]{1,0:T(8,128)(2,1)} %param.9) | copy-start | bytes 983044
  0.7 24.6 %copy-start.4 = (bf16[128,1280]{1,0:T(8,128)(2,1)S(1)}, bf16[128,1280]{1,0:T(8,128)(2,1)}, u32[]{:S(2)}) copy-start(bf16[128,1280]{1,0:T(8,128)(2,1)} %param.11) | copy-start | bytes 983044
  3.2 35.5 %copy-start.5 = (bf16[128,1280]{1,0:T(8,128)(2,1)S(1)}, bf16[128,1280]{1,0:T(8,128)(2,1)}, u32[]{:S(2)}) copy-start(bf16[128,1280]{1,0:T(8,128)(2,1)} %param.10) | copy-start | bytes 983044
  3.2 17.8 %all-to-all-start = ((bf16[16,8,1280]{2,1,0:T(8,128)(2,1)}), bf16[16,8,1280]{2,1,0:T(8,128)(2,1)S(1)}, u32[]{:S(2)}, u32[]{:S(2)}) async-start(bf16[16,8,1280]{2,1,0:T(8,128)(2,1)} %bitcast.1), calls=%async_computation | async-start | bytes 655360 | tf_op jit(solution)/shard_map/all_to_all | solution.py:86
  21.0 13.5 %all-to-all-start.2 = ((bf16[16,8,1280]{2,1,0:T(8,128)(2,1)}), bf16[16,8,1280]{2,1,0:T(8,128)(2,1)S(1)}, u32[]{:S(2)}, u32[]{:S(2)}) async-start(bf16[16,8,1280]{2,1,0:T(8,128)(2,1)} %bitcast.4), calls=%async_computation.2 | async-start | bytes 655360 | tf_op jit(solution)/shard_map/all_to_all | solution.py:87
  34.5 13.5 %all-to-all-start.4 = ((bf16[16,8,1280]{2,1,0:T(8,128)(2,1)}), bf16[16,8,1280]{2,1,0:T(8,128)(2,1)S(1)}, u32[]{:S(2)}, u32[]{:S(2)}) async-start(bf16[16,8,1280]{2,1,0:T(8,128)(2,1)} %bitcast.7), calls=%async_computation.4 | async-start | bytes 655360 | tf_op jit(solution)/shard_map/all_to_all | solution.py:89
  48.0 13.5 %all-to-all-start.6 = ((bf16[16,8,1280]{2,1,0:T(8,128)(2,1)}), bf16[16,8,1280]{2,1,0:T(8,128)(2,1)S(1)}, u32[]{:S(2)}, u32[]{:S(2)}) async-start(bf16[16,8,1280]{2,1,0:T(8,128)(2,1)} %bitcast.10), calls=%async_computation.6 | async-start | bytes 655360 | tf_op jit(solution)/shard_map/all_to_all | solution.py:88
  61.5 18.1 %all-to-all-start.1 = ((bf16[128,16,1,80]{0,3,2,1:T(8,128)(2,1)}), bf16[128,16,1,80]{0,3,2,1:T(8,128)(2,1)S(1)}, u32[]{:S(2)}, u32[]{:S(2)}) async-start(bf16[128,16,1,80]{0,3,2,1:T(8,128)(2,1)} %copy.43), calls=%async_computation.1 | async-start | bytes 655360 | tf_op jit(solution)/shard_map/all_to_all | solution.py:96
  79.6 15.3 %all-to-all-start.3 = ((bf16[128,16,1,80]{0,3,2,1:T(8,128)(2,1)}), bf16[128,16,1,80]{0,3,2,1:T(8,128)(2,1)S(1)}, u32[]{:S(2)}, u32[]{:S(2)}) async-start(bf16[128,16,1,80]{0,3,2,1:T(8,128)(2,1)} %copy.45), calls=%async_computation.3 | async-start | bytes 655360 | tf_op jit(solution)/shard_map/all_to_all | solution.py:97
  87.5 38.9 %copy-start.7 = (s32[1,2048]{1,0:T(1,128)S(1)}, s32[1,2048]{1,0:T(1,128)}, u32[]{:S(2)}) copy-start(s32[1,2048]{1,0:T(1,128)} %param.13) | copy-start | bytes 24580
  94.9 15.1 %all-to-all-start.5 = ((bf16[128,16,1,80]{0,3,2,1:T(8,128)(2,1)}), bf16[128,16,1,80]{0,3,2,1:T(8,128)(2,1)S(1)}, u32[]{:S(2)}, u32[]{:S(2)}) async-start(bf16[128,16,1,80]{0,3,2,1:T(8,128)(2,1)} %copy.47), calls=%async_computation.5 | async-start | bytes 655360 | tf_op jit(solution)/shard_map/all_to_all | solution.py:99
  110.0 15.4 %all-to-all-start.7 = ((bf16[128,16,1,80]{0,3,2,1:T(8,128)(2,1)}), bf16[128,16,1,80]{0,3,2,1:T(8,128)(2,1)S(1)}, u32[]{:S(2)}, u32[]{:S(2)}) async-start(bf16[128,16,1,80]{0,3,2,1:T(8,128)(2,1)} %copy.49), calls=%async_computation.7 | async-start | bytes 655360 | tf_op jit(solution)/shard_map/all_to_all | solution.py:98
  130.0 2.0 copy-start.1
  133.6 4.8 %copy-start.2 = (f32[512,2048]{1,0:T(8,128)S(1)}, f32[512,2048]{1,0:T(8,128)}, u32[]{:S(2)}) copy-start(f32[512,2048]{1,0:T(8,128)} %copy-done.1) | copy-start | bytes 12582916 | tf_op jit(solution)/shard_map/while
  143.5 2.0 copy-start.1
  147.1 5.0 %copy-start.2 = (f32[512,2048]{1,0:T(8,128)S(1)}, f32[512,2048]{1,0:T(8,128)}, u32[]{:S(2)}) copy-start(f32[512,2048]{1,0:T(8,128)} %copy-done.1) | copy-start | bytes 12582916 | tf_op jit(solution)/shard_map/while
  157.2 2.0 copy-start.1
  160.8 5.0 %copy-start.2 = (f32[512,2048]{1,0:T(8,128)S(1)}, f32[512,2048]{1,0:T(8,128)}, u32[]{:S(2)}) copy-start(f32[512,2048]{1,0:T(8,128)} %copy-done.1) | copy-start | bytes 12582916 | tf_op jit(solution)/shard_map/while
  170.9 2.0 copy-start.1
  174.5 5.0 %copy-start.2 = (f32[512,2048]{1,0:T(8,128)S(1)}, f32[512,2048]{1,0:T(8,128)}, u32[]{:S(2)}) copy-start(f32[512,2048]{1,0:T(8,128)} %copy-done.1) | copy-start | bytes 12582916 | tf_op jit(solution)/shard_map/while
  181.0 26.5 %copy-start.6 = (bf16[2048,1,80]{0,2,1:T(8,128)(2,1)S(1)}, bf16[2048,1,80]{0,2,1:T(8,128)(2,1)}, u32[]{:S(2)}) copy-start(bf16[2048,1,80]{0,2,1:T(8,128)(2,1)} %get-tuple-element.174) | copy-start | bytes 983044
  185.7 15.4 %all-to-all-start.12 = ((bf16[16,2,5120]{2,1,0:T(2,128)(2,1)}), bf16[16,2,5120]{2,1,0:T(2,128)(2,1)S(1)}, u32[]{:S(2)}, u32[]{:S(2)}) async-start(bf16[16,2,5120]{2,1,0:T(2,128)(2,1)} %reshape.200), calls=%async_computation.12 | async-start | bytes 655360 | tf_op jit(solution)/shard_map/all_to_all | solution.py:110
  201.1 15.4 %all-to-all-start.10 = ((bf16[16,2,5120]{2,1,0:T(2,128)(2,1)}), bf16[16,2,5120]{2,1,0:T(2,128)(2,1)S(1)}, u32[]{:S(2)}, u32[]{:S(2)}) async-start(bf16[16,2,5120]{2,1,0:T(2,128)(2,1)} %reshape.198), calls=%async_computation.10 | async-start | bytes 655360 | tf_op jit(solution)/shard_map/all_to_all | solution.py:107
  216.6 15.4 %all-to-all-start.8 = ((bf16[16,2,5120]{2,1,0:T(2,128)(2,1)}), bf16[16,2,5120]{2,1,0:T(2,128)(2,1)S(1)}, u32[]{:S(2)}, u32[]{:S(2)}) async-start(bf16[16,2,5120]{2,1,0:T(2,128)(2,1)} %reshape.196), calls=%async_computation.8 | async-start | bytes 655360 | tf_op jit(solution)/shard_map/all_to_all | solution.py:106
  232.0 16.8 %all-to-all-start.13 = ((bf16[16,8,1280]{2,1,0:T(8,128)(2,1)}), bf16[16,8,1280]{2,1,0:T(8,128)(2,1)S(1)}, u32[]{:S(2)}, u32[]{:S(2)}) async-start(bf16[16,8,1280]{2,1,0:T(8,128)(2,1)} %all_to_all.160), calls=%async_computation.13 | async-start | bytes 655360 | tf_op jit(solution)/shard_map/all_to_all | solution.py:122
  248.8 13.5 %all-to-all-start.11 = ((bf16[16,8,1280]{2,1,0:T(8,128)(2,1)}), bf16[16,8,1280]{2,1,0:T(8,128)(2,1)S(1)}, u32[]{:S(2)}, u32[]{:S(2)}) async-start(bf16[16,8,1280]{2,1,0:T(8,128)(2,1)} %all_to_all.154), calls=%async_computation.11 | async-start | bytes 655360 | tf_op jit(solution)/shard_map/all_to_all | solution.py:121
  262.3 13.5 %all-to-all-start.9 = ((bf16[16,8,1280]{2,1,0:T(8,128)(2,1)}), bf16[16,8,1280]{2,1,0:T(8,128)(2,1)S(1)}, u32[]{:S(2)}, u32[]{:S(2)}) async-start(bf16[16,8,1280]{2,1,0:T(8,128)(2,1)} %all_to_all.148), calls=%async_computation.9 | async-start | bytes 655360 | tf_op jit(solution)/shard_map/all_to_all | solution.py:120
where the time goes:
time: 280 us; the launch traced here: 277 us
  waiting for transfers between devices  92 us (33%)
  starting transfers between devices  83.5 us (30%)
  matrix products  47.1 us (17%)
  local copies, waits for them, and re-layouts  42.8 us (15%)
  other arithmetic  10.8 us (4%)
    dot_general x4, matrix products, visit(): jnp.einsum('hqk,qhd->khd', dscores, query_block, preferred_element_type=j...  10.2 us
    unnamed x24, local copies, waits for them, and re-layouts  9.88 us
    dot_general x4, matrix products, visit(): jnp.einsum('hqk,khd->qhd', dscores, key_rows, preferred_element_type=jnp....  9.5 us
    all_to_all x1, starting transfers between devices, on_device(): lax.all_to_all(permuted[0], 'dp', split_axis=0, concat_axis=0, tiled=True)  8.57 us
    all_to_all x1, starting transfers between devices, on_device(): lax.all_to_all(split_form[0], 'seq', split_axis=1, concat_axis=0, tiled=T...  8.4 us
    dot_general x4, matrix products, score_block(): jnp.einsum('qhd,khd->hqk', query_block, key_block, preferred_element_type...  7.88 us
    another operation x8, local copies, waits for them, and re-layouts, on_device(): item.reshape(rows, seq_devs, own_heads, HD)  7.82 us
    all_to_all x1, waiting for transfers between devices, on_device(): lax.all_to_all(split_form[0], 'seq', split_axis=1, concat_axis=0, tiled=T...  7.69 us
  transfers between devices with their start and end apart: 14, of which 14 were waited for; matrix products, arithmetic and copies ran while one was open for 12% of the time, Pallas kernels for 0%

commit v1 on v0

v1 whole, which is shorter than its diff:
```python
import functools
import math

import jax
import jax.numpy as jnp
from jax import lax
from jax.experimental import pallas as pl
from jax.experimental.pallas import tpu as pltpu
from jax.sharding import PartitionSpec as P

HD = 80
ROWS = 128
WIDTH = 1280
HALF = 640
SEQ = 16
GROUP = 2048
PAD = 128
MESH = pl.DeviceIdType.MESH
BIG = 1e30
INV_ROOT = 1.0 / math.sqrt(HD)
LOG2E_ROOT = INV_ROOT * math.log2(math.e)
TILE = 256
LOW, HIGH = 6, 10
BANDS = ((0, 3, 0, 5), (3, 5, 0, 8), (5, 8, 3, 8))
K, Q, G, V = 0, 1, 2, 3
GV, GQ, GK = 0, 1, 2
BF16 = jnp.bfloat16
F32 = jnp.float32


def dot_nn(a, b):
    return lax.dot_general(a, b, (((1,), (0,)), ((), ())), preferred_element_type=F32)


def dot_nt(a, b):
    return lax.dot_general(a, b, (((1,), (1,)), ((), ())), preferred_element_type=F32)


def identity(n):
    return (
        lax.broadcasted_iota(jnp.int32, (n, n), 0) == lax.broadcasted_iota(jnp.int32, (n, n), 1)
    ).astype(F32).astype(BF16)


def kernel(
    q_ref, k_ref, v_ref, g_ref, order_ref, seg_ref,
    gq_ref, gk_ref, gv_ref,
    send1, recv1, send2, recv2, send3, recv3, send4, recv4,
    rows_k, rows_v, extra, probs, score, order_t,
    s1, r1, s2, r2, s3, r3, s4, r4,
):
    dp = lax.axis_index("dp")
    seq = lax.axis_index("seq")
    y_lo = lax.div(seq, 8)
    z = lax.rem(seq, 8)
    core = lax.rem(dp, 2)
    x = lax.rem(lax.div(dp, 2), 4)
    y = lax.div(dp, 8) * 2 + y_lo

    def plane(k):
        pc = lax.rem(core + lax.rem(k, 2), 2)
        px = lax.rem(x + lax.rem(lax.div(k, 2), 4), 4)
        py = lax.rem(y + lax.div(k, 8), 4)
        return lax.div(py, 2) * 8 + px * 2 + pc, lax.rem(py, 2)

    def column(k):
        return lax.rem(z + k, 8)

    barrier = pltpu.get_barrier_semaphore()

    def greet_plane(k, c):
        pd, pyl = plane(k)
        pl.semaphore_signal(barrier, inc=1, device_id=(pd, pyl * 8 + z), device_id_type=MESH)
        return c

    lax.fori_loop(1, 32, greet_plane, 0)

    def greet_column(k, c):
        pl.semaphore_signal(
            barrier, inc=1, device_id=(dp, y_lo * 8 + column(k)), device_id_type=MESH
        )
        return c

    lax.fori_loop(1, 8, greet_column, 0)

    eye = identity(ROWS)
    onehot_t = (
        lax.broadcasted_iota(jnp.int32, (ROWS, ROWS), 0)
        == jnp.broadcast_to(order_ref[...], (ROWS, ROWS))
    ).astype(F32).astype(BF16)
    order_t[...] = onehot_t
    onehot = dot_nt(eye, onehot_t).astype(BF16)

    def permute(t, ref):
        for half in range(2):
            part = dot_nn(onehot, ref[:, half * HALF:(half + 1) * HALF])
            send1[t, half * 16:(half + 1) * 16] = part.reshape(16, 8, HALF).astype(BF16)

    def start1(t):
        own = y_lo * 16 + dp

        def one(k, c):
            pd, pyl = plane(k)
            pltpu.make_async_remote_copy(
                src_ref=send1.at[t, pyl * 16 + pd],
                dst_ref=recv1.at[t, own],
                send_sem=s1.at[t],
                recv_sem=r1.at[t],
                device_id=(pd, pyl * 8 + z),
                device_id_type=MESH,
            ).start()
            return c

        lax.fori_loop(1, 32, one, 0)
        pltpu.make_async_copy(send1.at[t, own], recv1.at[t, own], r1.at[t]).start()

    def start2(t):
        pltpu.make_async_copy(recv1.at[t], recv1.at[t], r1.at[t]).wait()
        for half in range(2):
            rows = recv1[t, half * 16:(half + 1) * 16].astype(F32).reshape(ROWS, HALF).astype(BF16)
            for c in range(5):
                part = dot_nt(eye, rows[:, c * 128:(c + 1) * 128]).astype(BF16)
                send2[t, half, c * 128:(c + 1) * 128] = part
        for half in range(2):
            for k in (1, 7, 2, 6, 3, 5, 4):
                pz = column(k)
                pltpu.make_async_remote_copy(
                    src_ref=send2.at[t, half, pl.ds(pl.multiple_of(pz * HD, 16), HD)],
                    dst_ref=recv2.at[t, half * 8 + z],
                    send_sem=s2.at[t],
                    recv_sem=r2.at[t],
                    device_id=(dp, y_lo * 8 + pz),
                    device_id_type=MESH,
                ).start()
            pltpu.make_async_copy(
                send2.at[t, half, pl.ds(pl.multiple_of(z * HD, 16), HD)],
                recv2.at[t, half * 8 + z],
                r2.at[t],
            ).start()

    def arrived2(t):
        pltpu.make_async_copy(recv2.at[t], recv2.at[t], r2.at[t]).wait()

    def wide(t, first, last):
        return jnp.concatenate([recv2[t, s] for s in range(first, last)], axis=1)

    permute(K, k_ref)
    pl.semaphore_wait(barrier, 38)
    start1(K)
    permute(Q, q_ref)
    start1(Q)
    permute(G, g_ref)
    permute(V, v_ref)

    index = lax.broadcasted_iota(jnp.int32, (PAD - HD, GROUP), 0)
    seg = jnp.broadcast_to(seg_ref[...].astype(F32), (PAD - HD, GROUP))
    first, second = index == 0, index == 1
    extra[0] = jnp.where(first, seg, jnp.where(second, 1.0 - seg, 0.0)).astype(BF16)
    extra[1] = jnp.where(first, -BIG * (1.0 - seg), jnp.where(second, -BIG * seg, 0.0)).astype(BF16)

    start2(K)
    start1(G)
    start2(Q)
    start1(V)
    start2(G)

    arrived2(K)
    for s in range(SEQ):
        full = jnp.concatenate([recv2[K, s], extra[0, :, s * ROWS:(s + 1) * ROWS]], axis=0)
        rows_k[s * ROWS:(s + 1) * ROWS] = dot_nt(eye, full).astype(BF16)
    start2(V)
    arrived2(Q)

    for q_first, q_last, k_first, k_last in BANDS:

        def soft_tile(qt, c, k_first=k_first, k_last=k_last):
            lanes = pl.ds(pl.multiple_of(qt * TILE, TILE), TILE)
            q_t = jnp.concatenate(
                [
                    jnp.concatenate([recv2[Q, 2 * qt], recv2[Q, 2 * qt + 1]], axis=1),
                    extra[1, :, lanes],
                ],
                axis=0,
            )
            top = jnp.full((8, TILE), -jnp.inf, F32)
            for kt in range(k_first, k_last):
                part = dot_nn(rows_k[kt * TILE:(kt + 1) * TILE], q_t)
                score[kt * TILE:(kt + 1) * TILE] = part
                top = jnp.maximum(top, jnp.max(part.reshape(TILE // 8, 8, TILE), axis=0))
            top = jnp.max(top, axis=0, keepdims=True) * LOG2E_ROOT
            total = jnp.zeros((8, TILE), F32)
            for kt in range(k_first, k_last):
                part = jnp.exp2(score[kt * TILE:(kt + 1) * TILE] * LOG2E_ROOT - top)
                score[kt * TILE:(kt + 1) * TILE] = part
                total = total + jnp.sum(part.reshape(TILE // 8, 8, TILE), axis=0)
            scale = 1.0 / jnp.sum(total, axis=0, keepdims=True)
            for kt in range(k_first, k_last):
                probs[kt * TILE:(kt + 1) * TILE, lanes] = (
                    score[kt * TILE:(kt + 1) * TILE] * scale
                ).astype(BF16)
            return c

        lax.fori_loop(q_first, q_last, soft_tile, 0)

    def start3(t, s, unroll_z=None):
        pz = lax.rem(s, 8)
        half = lax.div(s, 8)

        @pl.when(pz != z)
        def _():
            pltpu.make_async_remote_copy(
                src_ref=send3.at[t, s],
                dst_ref=recv3.at[t, half, pl.ds(pl.multiple_of(z * HD, 16), HD)],
                send_sem=s3.at[t],
                recv_sem=r3.at[t],
                device_id=(dp, y_lo * 8 + pz),
                device_id_type=MESH,
            ).start()

        @pl.when(pz == z)
        def _():
            pltpu.make_async_copy(
                send3.at[t, s],
                recv3.at[t, half, pl.ds(pl.multiple_of(z * HD, 16), HD)],
                r3.at[t],
            ).start()

    def key_side(t, source, scale):
        for k_first, k_last, q_first, q_last in BANDS:
            left = wide(source, 2 * q_first, 2 * q_last)
            for kt in range(k_first, k_last):
                part = dot_nt(
                    left, probs[kt * TILE:(kt + 1) * TILE, q_first * TILE:q_last * TILE]
                )
                part = (part * scale).astype(BF16)
                send3[t, 2 * kt] = part[:, :ROWS]
                send3[t, 2 * kt + 1] = part[:, ROWS:]

    def start3_all(t):
        def one(i, c):
            start3(t, lax.rem(lax.div(i, 2) + z + 1, 8) + 8 * lax.rem(i, 2))
            return c

        lax.fori_loop(0, SEQ, one, 0)

    arrived2(G)
    key_side(GV, G, 1.0)
    start3_all(GV)

    arrived2(V)
    for s in range(SEQ):
        full = jnp.concatenate([recv2[V, s], jnp.zeros((PAD - HD, ROWS), BF16)], axis=0)
        rows_v[s * ROWS:(s + 1) * ROWS] = dot_nt(eye, full).astype(BF16)

    for q_first, q_last, k_first, k_last in BANDS:
        k_wide = wide(K, 2 * k_first, 2 * k_last)

        def grad_tile(qt, c, k_first=k_first, k_last=k_last, k_wide=k_wide):
            lanes = pl.ds(pl.multiple_of(qt * TILE, TILE), TILE)
            g_t = jnp.concatenate(
                [
                    jnp.concatenate([recv2[G, 2 * qt], recv2[G, 2 * qt + 1]], axis=1),
                    jnp.zeros((PAD - HD, TILE), BF16),
                ],
                axis=0,
            )
            delta = jnp.zeros((8, TILE), F32)
            for kt in range(k_first, k_last):
                part = dot_nn(rows_v[kt * TILE:(kt + 1) * TILE], g_t)
                score[kt * TILE:(kt + 1) * TILE] = part
                weighed = part * probs[kt * TILE:(kt + 1) * TILE, lanes].astype(F32)
                delta = delta + jnp.sum(weighed.reshape(TILE // 8, 8, TILE), axis=0)
            delta = jnp.sum(delta, axis=0, keepdims=True)
            for kt in range(k_first, k_last):
                part = score[kt * TILE:(kt + 1) * TILE] - delta
                part = part * probs[kt * TILE:(kt + 1) * TILE, lanes].astype(F32)
                probs[kt * TILE:(kt + 1) * TILE, lanes] = part.astype(BF16)
            grad = dot_nn(k_wide, probs[k_first * TILE:k_last * TILE, lanes]) * INV_ROOT
            grad = grad.astype(BF16)
            send3[GQ, 2 * qt] = grad[:, :ROWS]
            send3[GQ, 2 * qt + 1] = grad[:, ROWS:]
            return c

        lax.fori_loop(q_first, q_last, grad_tile, 0)

    start3_all(GQ)
    key_side(GK, Q, INV_ROOT)
    start3_all(GK)

    def start4(t):
        pltpu.make_async_copy(recv3.at[t], recv3.at[t], r3.at[t]).wait()
        own = y_lo * 16 + dp
        for half in range(2):
            for c in range(5):
                part = dot_nt(eye, recv3[t, half, c * 128:(c + 1) * 128])
                send4[t, half * 16:(half + 1) * 16, :, c * 128:(c + 1) * 128] = part.reshape(
                    16, 8, 128
                ).astype(BF16)

        def one(k, c):
            pd, pyl = plane(k)
            pltpu.make_async_remote_copy(
                src_ref=send4.at[t, pyl * 16 + pd],
                dst_ref=recv4.at[t, own],
                send_sem=s4.at[t],
                recv_sem=r4.at[t],
                device_id=(pd, pyl * 8 + z),
                device_id_type=MESH,
            ).start()
            return c

        lax.fori_loop(1, 32, one, 0)
        pltpu.make_async_copy(send4.at[t, own], recv4.at[t, own], r4.at[t]).start()

    def finish(t, ref):
        pltpu.make_async_copy(recv4.at[t], recv4.at[t], r4.at[t]).wait()
        for half in range(2):
            rows = recv4[t, half * 16:(half + 1) * 16].astype(F32).reshape(ROWS, HALF).astype(BF16)
            ref[:, half * HALF:(half + 1) * HALF] = dot_nn(order_t[...], rows).astype(BF16)

    start4(GV)
    start4(GQ)
    finish(GV, gv_ref)
    start4(GK)
    finish(GQ, gq_ref)
    finish(GK, gk_ref)

    for t in range(4):
        pltpu.make_async_copy(
            send1.at[t, pl.ds(0, 31)], send1.at[t, pl.ds(0, 31)], s1.at[t]
        ).wait()
        pltpu.make_async_copy(
            recv2.at[t, pl.ds(0, 14)], recv2.at[t, pl.ds(0, 14)], s2.at[t]
        ).wait()
    for t in range(3):
        pltpu.make_async_copy(
            send3.at[t, pl.ds(0, 14)], send3.at[t, pl.ds(0, 14)], s3.at[t]
        ).wait()
        pltpu.make_async_copy(
            send4.at[t, pl.ds(0, 31)], send4.at[t, pl.ds(0, 31)], s4.at[t]
        ).wait()


def on_device(queries, key_states, value_states, out_grads, row_order, segment_ids):
    out = jax.ShapeDtypeStruct((ROWS, WIDTH), BF16)
    vmem = pl.BlockSpec(memory_space=pltpu.VMEM)
    grads = pl.pallas_call(
        kernel,
        out_shape=(out, out, out),
        in_specs=[vmem] * 6,
        out_specs=(vmem, vmem, vmem),
        scratch_shapes=[
            pltpu.VMEM((4, 32, 8, HALF), BF16),
            pltpu.VMEM((4, 32, 8, HALF), BF16),
            pltpu.VMEM((4, 2, HALF, ROWS), BF16),
            pltpu.VMEM((4, SEQ, HD, ROWS), BF16),
            pltpu.VMEM((3, SEQ, HD, ROWS), BF16),
            pltpu.VMEM((3, 2, HALF, ROWS), BF16),
            pltpu.VMEM((3, 32, 8, HALF), BF16),
            pltpu.VMEM((3, 32, 8, HALF), BF16),
            pltpu.VMEM((GROUP, PAD), BF16),
            pltpu.VMEM((GROUP, PAD), BF16),
            pltpu.VMEM((2, PAD - HD, GROUP), BF16),
            pltpu.VMEM((GROUP, GROUP), BF16),
            pltpu.VMEM((GROUP, TILE), F32),
            pltpu.VMEM((ROWS, ROWS), BF16),
            pltpu.SemaphoreType.DMA((4,)),
            pltpu.SemaphoreType.DMA((4,)),
            pltpu.SemaphoreType.DMA((4,)),
            pltpu.SemaphoreType.DMA((4,)),
            pltpu.SemaphoreType.DMA((3,)),
            pltpu.SemaphoreType.DMA((3,)),
            pltpu.SemaphoreType.DMA((3,)),
            pltpu.SemaphoreType.DMA((3,)),
        ],
        compiler_params=pltpu.CompilerParams(collective_id=0, has_side_effects=True),
    )(queries, key_states, value_states, out_grads, row_order[None, :], segment_ids)
    return grads


def solution(mesh):
    rows = P(("dp", "seq"), None)
    return jax.shard_map(
        on_device,
        mesh=mesh,
        in_specs=(rows, rows, rows, rows, P(("dp", "seq")), P("dp", None)),
        out_specs=(rows, rows, rows),
        check_vma=False,
    )
```

time: 280 us -> 89.7 us (0.32)
  waiting for transfers between devices: 92 us -> 0 us
  Pallas kernels: 0 us -> 85 us
  starting transfers between devices: 83.5 us -> 0 us
  matrix products: 47.1 us -> 0 us
  local copies, waits for them, and re-layouts: 42.8 us -> 3.58 us
  other arithmetic: 10.8 us -> 0 us
    all_to_all x14 -> x0, waiting for transfers between devices: 92 us -> none  [the longest x1 7.69 us: on_device(): lax.all_to_all(split_form[0], 'seq', split_axis=1, concat_axis=0, tiled=T...]
    pallas_call x0 -> x1, Pallas kernels: none -> 85 us  [on_device(): pl.pallas_call(kernel, out_shape=(out, out, out), in_specs=[vmem] * 6, ou...]
    all_to_all x14 -> x0, starting transfers between devices: 83.5 us -> none  [the longest x1 8.57 us: on_device(): lax.all_to_all(permuted[0], 'dp', split_axis=0, concat_axis=0, tiled=True)]
    dot_general x24 -> x0, matrix products: 47.1 us -> none  [the longest x4 10.2 us: visit(): jnp.einsum('hqk,qhd->khd', dscores, query_block, preferred_element_type=j...]
    gather x7 -> x0, local copies, waits for them, and re-layouts: 11.3 us -> none  [the longest x3 4.84 us: on_device(): return (returned[0][inverse], returned[1][inverse], returned[2][inverse])]
    another operation x8 -> x0, local copies, waits for them, and re-layouts: 7.82 us -> none  [on_device(): item.reshape(rows, seq_devs, own_heads, HD)]
    all_to_all x13 -> x0, local copies, waits for them, and re-layouts: 7.74 us -> none  [the longest x1 1.27 us: on_device(): lax.all_to_all(flat[2], 'dp', split_axis=0, concat_axis=0, tiled=True)]
    unnamed x24 -> x7, local copies, waits for them, and re-layouts: 9.88 us -> 3.58 us
  transfers between devices with their start and end apart: 14 -> 0, of which waited for: 14 -> 0; matrix products, arithmetic and copies ran while one was open for 12% -> 0% of each run, Pallas kernels for 0% -> 0%
where the time goes in v1:
time: 89.7 us; the launch traced here: 89.3 us
  Pallas kernels  85 us (95%)
  local copies, waits for them, and re-layouts  3.58 us (4%)
    pallas_call x1, Pallas kernels, on_device(): pl.pallas_call(kernel, out_shape=(out, out, out), in_specs=[vmem] * 6, ou...  85 us
    unnamed x7, local copies, waits for them, and re-layouts  3.58 us

profile of v1, /device:TPU:1, one launch (start us, length us, event | category | flops | bytes accessed | tf_op | source)
XLA Modules:
  0.0 89.3 jit_solution(14509338314959656071)
XLA Ops:
  0.6 85.0 %shard_map.85 = (bf16[128,1280]{1,0:T(8,128)(2,1)}, bf16[128,1280]{1,0:T(8,128)(2,1)}, bf16[128,1280]{1,0:T(8,128)(2,1)}) custom-call(bf16[128,1280]{1,0:T(8,128)(2,1)} %q_ref.1, bf16[128,1280]{1,0:T(8,128)(2,1)} %k_ref.1, bf16[128,1280]{1,0:T(8,128)(2,1)} %v_ref.1, bf16[128,1280]{1,0:T(8,128)(2,1)} %g_ref.1, s32[1,128]{1,0:T(1,128)} %bitcast.1, ...), custom_call_target="tpu_custom_call" | custom-call | tf_op jit(solution)/shard_map/pallas_call | solution.py:347
  85.7 0.0 copy-start.1
  85.7 1.8 %copy.12 = bf16[128,1280]{1,0:T(8,128)(2,1)} copy(bf16[128,1280]{1,0:T(8,128)(2,1)} %get-tuple-element.6) | data formatting | bytes 655360
  87.4 0.0 copy-done.1
  87.4 0.0 copy-start
  87.4 0.7 copy.13
  88.2 0.4 copy-done
  88.5 0.7 copy.14
Async XLA Ops:
  85.7 1.8 %copy-start.1 = (bf16[128,1280]{1,0:T(8,128)(2,1)S(1)}, bf16[128,1280]{1,0:T(8,128)(2,1)}, u32[]{:S(2)}) copy-start(bf16[128,1280]{1,0:T(8,128)(2,1)} %get-tuple-element.7) | copy-start | bytes 983044
  87.4 1.1 %copy-start = (bf16[128,1280]{1,0:T(8,128)(2,1)S(1)}, bf16[128,1280]{1,0:T(8,128)(2,1)}, u32[]{:S(2)}) copy-start(bf16[128,1280]{1,0:T(8,128)(2,1)} %get-tuple-element.8) | copy-start | bytes 983044

commit v2 on v1

v2 whole, which is shorter than its diff:
```python
import functools
import math

import jax
import jax.numpy as jnp
from jax import lax
from jax.experimental import pallas as pl
from jax.experimental.pallas import tpu as pltpu
from jax.sharding import PartitionSpec as P

HD = 80
ROWS = 128
WIDTH = 1280
HALF = 640
SEQ = 16
GROUP = 2048
PAD = 128
MESH = pl.DeviceIdType.MESH
BIG = 1e30
INV_ROOT = 1.0 / math.sqrt(HD)
LOG2E_ROOT = INV_ROOT * math.log2(math.e)
TILE = 256
LOW, HIGH = 6, 10
BANDS = ((0, 3, 0, 5), (3, 5, 0, 8), (5, 8, 3, 8))
K, Q, G, V = 0, 1, 2, 3
GV, GQ, GK = 0, 1, 2
BF16 = jnp.bfloat16
F32 = jnp.float32


def dot_nn(a, b):
    return lax.dot_general(a, b, (((1,), (0,)), ((), ())), preferred_element_type=F32)


def dot_nt(a, b):
    return lax.dot_general(a, b, (((1,), (1,)), ((), ())), preferred_element_type=F32)


def identity(n):
    return (
        lax.broadcasted_iota(jnp.int32, (n, n), 0) == lax.broadcasted_iota(jnp.int32, (n, n), 1)
    ).astype(F32).astype(BF16)


def scope(name):
    return jax.named_scope(name)


def onehot_of(order_row):
    return (
        lax.broadcasted_iota(jnp.int32, (ROWS, ROWS), 0)
        == jnp.broadcast_to(order_row, (ROWS, ROWS))
    ).astype(F32).astype(BF16)


def put_back(onehot_t, blocks, ref):
    for half in range(2):
        rows = blocks[half].astype(F32).reshape(ROWS, HALF).astype(BF16)
        ref[:, half * HALF:(half + 1) * HALF] = dot_nn(onehot_t, rows).astype(BF16)


def kernel(
    q_hbm, k_hbm, v_hbm, g_hbm, order_hbm, seg_hbm,
    gv_ref, gq_ref, raw_ref,
    held, order_ref, seg_ref,
    send1, recv1, send2, recv2, send3, recv3, send4, recv4,
    rows_k, rows_v, extra, probs, score, order_t,
    load, s1, r1, s2, r2, s3, r3, s4, r4,
):
    dp = lax.axis_index("dp")
    seq = lax.axis_index("seq")
    y_lo = lax.div(seq, 8)
    z = lax.rem(seq, 8)
    core = lax.rem(dp, 2)
    x = lax.rem(lax.div(dp, 2), 4)
    y_hi = lax.div(dp, 8)
    other = 1 - y_lo

    def near(k):
        pc = lax.rem(core + lax.div(k, 8), 2)
        px = lax.rem(x + lax.rem(lax.div(k, 2), 4), 4)
        return lax.rem(y_hi + lax.rem(k, 2), 2) * 8 + px * 2 + pc

    def column(k):
        return lax.rem(z + k, 8)

    barrier = pltpu.get_barrier_semaphore()

    def greet(device):
        pl.semaphore_signal(barrier, inc=1, device_id=device, device_id_type=MESH)

    def greet_plane(k, c):
        pd = near(k)
        greet((pd, other * 8 + z))

        @pl.when(k > 0)
        def _():
            greet((pd, seq))

        return c

    def greet_column(k, c):
        greet((dp, y_lo * 8 + column(k)))
        return c

    loads = [
        pltpu.make_async_copy(src, dst, load.at[i])
        for i, (src, dst) in enumerate(
            [(order_hbm, order_ref)]
            + [(ref, held.at[t]) for t, ref in enumerate((k_hbm, q_hbm, g_hbm, v_hbm))]
            + [(seg_hbm, seg_ref)]
        )
    ]
    for copy in loads:
        copy.start()
    with scope("A_greet"):
        lax.fori_loop(1, 8, greet_column, 0)
        lax.fori_loop(0, 16, greet_plane, 0)

    eye = identity(ROWS)

    def permute(t, onehot):
        loads[1 + t].wait()
        for half in range(2):
            part = dot_nn(onehot, held[t, :, half * HALF:(half + 1) * HALF])
            send1[t, half] = part.reshape(16, 8, HALF).astype(BF16)

    def start1(t, half_is_other):
        half = other if half_is_other else y_lo

        def one(k, c):
            pd = near(k)
            pltpu.make_async_remote_copy(
                src_ref=send1.at[t, half, pd],
                dst_ref=recv1.at[t, y_lo, dp],
                send_sem=s1.at[t],
                recv_sem=r1.at[t, 0 if half_is_other else 1],
                device_id=(pd, half * 8 + z),
                device_id_type=MESH,
            ).start()
            return c

        lax.fori_loop(0 if half_is_other else 1, 16, one, 0)
        if not half_is_other:
            pltpu.make_async_copy(
                send1.at[t, half, dp], recv1.at[t, half, dp], r1.at[t, 1]
            ).start()

    def start2(t, half_is_other):
        half = other if half_is_other else y_lo
        with scope("wait1"):
            pltpu.make_async_copy(
                recv1.at[t, half], recv1.at[t, half], r1.at[t, 0 if half_is_other else 1]
            ).wait()
        rows = recv1[t, half].astype(F32).reshape(ROWS, HALF).astype(BF16)
        for c in range(5):
            part = dot_nt(eye, rows[:, c * 128:(c + 1) * 128]).astype(BF16)
            send2[t, half, c * 128:(c + 1) * 128] = part
        for k in (1, 7, 2, 6, 3, 5, 4):
            pz = column(k)
            pltpu.make_async_remote_copy(
                src_ref=send2.at[t, half, pl.ds(pl.multiple_of(pz * HD, 16), HD)],
                dst_ref=recv2.at[t, half * 8 + z],
                send_sem=s2.at[t],
                recv_sem=r2.at[t],
                device_id=(dp, y_lo * 8 + pz),
                device_id_type=MESH,
            ).start()
        pltpu.make_async_copy(
            send2.at[t, half, pl.ds(pl.multiple_of(z * HD, 16), HD)],
            recv2.at[t, half * 8 + z],
            r2.at[t],
        ).start()

    def arrived2(t):
        with scope("wait2"):
            pltpu.make_async_copy(recv2.at[t], recv2.at[t], r2.at[t]).wait()

    def wide(t, first, last):
        return jnp.concatenate([recv2[t, s] for s in range(first, last)], axis=1)

    with scope("A_perm"):
        loads[0].wait()
        onehot_t = onehot_of(order_ref[...])
        order_t[...] = onehot_t
        onehot = dot_nt(eye, onehot_t).astype(BF16)
        for t in (K, Q, G, V):
            permute(t, onehot)

    with scope("A_extra"):
        loads[5].wait()
        index = lax.broadcasted_iota(jnp.int32, (PAD - HD, GROUP), 0)
        seg = jnp.broadcast_to(seg_ref[...].astype(F32), (PAD - HD, GROUP))
        first, second = index == 0, index == 1
        extra[0] = jnp.where(first, seg, jnp.where(second, 1.0 - seg, 0.0)).astype(BF16)
        extra[1] = jnp.where(
            first, -BIG * (1.0 - seg), jnp.where(second, -BIG * seg, 0.0)
        ).astype(BF16)

    with scope("A_barrier"):
        pl.semaphore_wait(barrier, 38)
    with scope("A_start1K"):
        start1(K, True)
        start1(K, False)
    with scope("B_start2K"):
        start2(K, True)
    with scope("A_start1Q"):
        start1(Q, True)
        start1(Q, False)
    with scope("B_start2K"):
        start2(K, False)
    with scope("B_start2Q"):
        start2(Q, True)
    with scope("B_start1G"):
        start1(G, True)
        start1(G, False)
    with scope("B_start2Q"):
        start2(Q, False)
    with scope("B_start1V"):
        start1(V, True)
        start1(V, False)
    with scope("B_start2G"):
        start2(G, True)
        start2(G, False)

    arrived2(K)
    for s in range(SEQ):
        full = jnp.concatenate([recv2[K, s], extra[0, :, s * ROWS:(s + 1) * ROWS]], axis=0)
        rows_k[s * ROWS:(s + 1) * ROWS] = dot_nt(eye, full).astype(BF16)
    with scope("B_start2V"):
        start2(V, True)
        start2(V, False)
    arrived2(Q)

    for q_first, q_last, k_first, k_last in BANDS:

        def soft_tile(qt, c, k_first=k_first, k_last=k_last):
            lanes = pl.ds(pl.multiple_of(qt * TILE, TILE), TILE)
            q_t = jnp.concatenate(
                [
                    jnp.concatenate([recv2[Q, 2 * qt], recv2[Q, 2 * qt + 1]], axis=1),
                    extra[1, :, lanes],
                ],
                axis=0,
            )
            top = jnp.full((8, TILE), -jnp.inf, F32)
            for kt in range(k_first, k_last):
                part = dot_nn(rows_k[kt * TILE:(kt + 1) * TILE], q_t)
                score[kt * TILE:(kt + 1) * TILE] = part
                top = jnp.maximum(top, jnp.max(part.reshape(TILE // 8, 8, TILE), axis=0))
            top = jnp.max(top, axis=0, keepdims=True) * LOG2E_ROOT
            total = jnp.zeros((8, TILE), F32)
            for kt in range(k_first, k_last):
                part = jnp.exp2(score[kt * TILE:(kt + 1) * TILE] * LOG2E_ROOT - top)
                score[kt * TILE:(kt + 1) * TILE] = part
                total = total + jnp.sum(part.reshape(TILE // 8, 8, TILE), axis=0)
            scale = 1.0 / jnp.sum(total, axis=0, keepdims=True)
            for kt in range(k_first, k_last):
                probs[kt * TILE:(kt + 1) * TILE, lanes] = (
                    score[kt * TILE:(kt + 1) * TILE] * scale
                ).astype(BF16)
            return c

        with scope("C_soft"):
            lax.fori_loop(q_first, q_last, soft_tile, 0)

    def start3(t, half, pz, which):
        s = half * 8 + pz
        dst = recv3.at[t, half, pl.ds(pl.multiple_of(z * HD, 16), HD)]

        @pl.when(pz != z)
        def _():
            pltpu.make_async_remote_copy(
                src_ref=send3.at[t, s],
                dst_ref=dst,
                send_sem=s3.at[t],
                recv_sem=r3.at[t, which],
                device_id=(dp, y_lo * 8 + pz),
                device_id_type=MESH,
            ).start()

        @pl.when(pz == z)
        def _():
            pltpu.make_async_copy(send3.at[t, s], dst, r3.at[t, which]).start()

    def key_side(t, source, scale):
        for k_first, k_last, q_first, q_last in BANDS:
            left = wide(source, 2 * q_first, 2 * q_last)
            for kt in range(k_first, k_last):
                part = dot_nt(
                    left, probs[kt * TILE:(kt + 1) * TILE, q_first * TILE:q_last * TILE]
                )
                part = (part * scale).astype(BF16)
                send3[t, 2 * kt] = part[:, :ROWS]
                send3[t, 2 * kt + 1] = part[:, ROWS:]

    def start3_all(t):
        for which, half in ((0, y_lo), (1, other)):

            def one(k, c, which=which, half=half):
                start3(t, half, column(k), which)
                return c

            lax.fori_loop(1, 9, one, 0)

    arrived2(G)
    with scope("C_gv"):
        key_side(GV, G, 1.0)
    with scope("C_start3"):
        start3_all(GV)

    arrived2(V)
    for s in range(SEQ):
        full = jnp.concatenate([recv2[V, s], jnp.zeros((PAD - HD, ROWS), BF16)], axis=0)
        rows_v[s * ROWS:(s + 1) * ROWS] = dot_nt(eye, full).astype(BF16)

    def grad_tile(qt, k_first, k_last):
        lanes = pl.ds(pl.multiple_of(qt * TILE, TILE), TILE)
        g_t = jnp.concatenate(
            [
                jnp.concatenate([recv2[G, 2 * qt], recv2[G, 2 * qt + 1]], axis=1),
                jnp.zeros((PAD - HD, TILE), BF16),
            ],
            axis=0,
        )
        delta = jnp.zeros((8, TILE), F32)
        for kt in range(k_first, k_last):
            part = dot_nn(rows_v[kt * TILE:(kt + 1) * TILE], g_t)
            score[kt * TILE:(kt + 1) * TILE] = part
            weighed = part * probs[kt * TILE:(kt + 1) * TILE, lanes].astype(F32)
            delta = delta + jnp.sum(weighed.reshape(TILE // 8, 8, TILE), axis=0)
        delta = jnp.sum(delta, axis=0, keepdims=True)
        for kt in range(k_first, k_last):
            part = score[kt * TILE:(kt + 1) * TILE] - delta
            part = part * probs[kt * TILE:(kt + 1) * TILE, lanes].astype(F32)
            probs[kt * TILE:(kt + 1) * TILE, lanes] = part.astype(BF16)
        k_wide = wide(K, 2 * k_first, 2 * k_last)
        grad = dot_nn(k_wide, probs[k_first * TILE:k_last * TILE, lanes]) * INV_ROOT
        grad = grad.astype(BF16)
        send3[GQ, 2 * qt] = grad[:, :ROWS]
        send3[GQ, 2 * qt + 1] = grad[:, ROWS:]

    def grad_step(i, c):
        pair = lax.rem(lax.div(z, 2) + 1 + lax.div(i, 2), 4)
        half = lax.rem(i, 2)
        qt = pair + 4 * half
        for q_first, q_last, k_first, k_last in BANDS:

            @pl.when(jnp.logical_and(qt >= q_first, qt < q_last))
            def _(k_first=k_first, k_last=k_last):
                grad_tile(qt, k_first, k_last)

        for j in range(2):
            for which, mine in ((0, half == y_lo), (1, half != y_lo)):

                @pl.when(mine)
                def _(j=j, which=which):
                    start3(GQ, half, 2 * pair + j, which)

        return c

    with scope("D_grad"):
        lax.fori_loop(0, 8, grad_step, 0)
    def start4(t, which):
        half = other if which else y_lo
        with scope("wait3"):
            pltpu.make_async_copy(
                recv3.at[t, half], recv3.at[t, half], r3.at[t, which]
            ).wait()
        for c in range(5):
            part = dot_nt(eye, recv3[t, half, c * 128:(c + 1) * 128])
            send4[t, half, :, :, c * 128:(c + 1) * 128] = part.reshape(16, 8, 128).astype(BF16)

        def one(k, c):
            pd = near(k)
            pltpu.make_async_remote_copy(
                src_ref=send4.at[t, half, pd],
                dst_ref=(raw_ref if t == GK else recv4.at[t]).at[y_lo, dp],
                send_sem=s4.at[t],
                recv_sem=r4.at[t],
                device_id=(pd, half * 8 + z),
                device_id_type=MESH,
            ).start()
            return c

        lax.fori_loop(0 if which else 1, 16, one, 0)
        if not which:
            pltpu.make_async_copy(
                send4.at[t, half, dp],
                (raw_ref if t == GK else recv4.at[t]).at[half, dp],
                r4.at[t],
            ).start()

    with scope("E_start4V"):
        start4(GV, 0)
        start4(GV, 1)
    with scope("D_gk"):
        key_side(GK, Q, INV_ROOT)
    start3_all(GK)

    def finish(t, ref):
        with scope("wait4"):
            pltpu.make_async_copy(recv4.at[t], recv4.at[t], r4.at[t]).wait()
        put_back(order_t[...], recv4[t], ref)

    with scope("E_start4Q"):
        start4(GQ, 0)
        start4(GQ, 1)
    with scope("E_start4K0"):
        start4(GK, 0)
    with scope("E_start4K1"):
        start4(GK, 1)
    with scope("E_finV"):
        finish(GV, gv_ref)
    with scope("E_finQ"):
        finish(GQ, gq_ref)

    with scope("E_sent"):
        for t in range(4):
            for half in range(2):
                part = send1.at[t, half, pl.ds(0, 16 - half)]
                pltpu.make_async_copy(part, part, s1.at[t]).wait()
            part = recv2.at[t, pl.ds(0, 14)]
            pltpu.make_async_copy(part, part, s2.at[t]).wait()
        for t in range(3):
            part = send3.at[t, pl.ds(0, 14)]
            pltpu.make_async_copy(part, part, s3.at[t]).wait()
            for half in range(2):
                part = send4.at[t, half, pl.ds(0, 16 - half)]
                pltpu.make_async_copy(part, part, s4.at[t]).wait()
    with scope("E_last"):
        pltpu.make_async_copy(raw_ref, raw_ref, r4.at[GK]).wait()


def last_kernel(gv_ref, gq_ref, raw_ref, order_ref, gq_out, gk_out, gv_out):
    put_back(onehot_of(order_ref[...]), raw_ref[...], gk_out)
    gv_out[...] = gv_ref[...]
    gq_out[...] = gq_ref[...]


def on_device(queries, key_states, value_states, out_grads, row_order, segment_ids):
    out = jax.ShapeDtypeStruct((ROWS, WIDTH), BF16)
    raw = jax.ShapeDtypeStruct((2, 16, 8, HALF), BF16)
    vmem = pl.BlockSpec(memory_space=pltpu.VMEM)
    anywhere = pl.BlockSpec(memory_space=pl.ANY)
    order = row_order[None, :]
    parts = pl.pallas_call(
        kernel,
        out_shape=(out, out, raw),
        in_specs=[anywhere] * 6,
        out_specs=(vmem, vmem, vmem),
        scratch_shapes=[
            pltpu.VMEM((4, ROWS, WIDTH), BF16),
            pltpu.VMEM((1, ROWS), jnp.int32),
            pltpu.VMEM((1, GROUP), jnp.int32),
            pltpu.VMEM((4, 2, 16, 8, HALF), BF16),
            pltpu.VMEM((4, 2, 16, 8, HALF), BF16),
            pltpu.VMEM((4, 2, HALF, ROWS), BF16),
            pltpu.VMEM((4, SEQ, HD, ROWS), BF16),
            pltpu.VMEM((3, SEQ, HD, ROWS), BF16),
            pltpu.VMEM((3, 2, HALF, ROWS), BF16),
            pltpu.VMEM((3, 2, 16, 8, HALF), BF16),
            pltpu.VMEM((2, 2, 16, 8, HALF), BF16),
            pltpu.VMEM((GROUP, PAD), BF16),
            pltpu.VMEM((GROUP, PAD), BF16),
            pltpu.VMEM((2, PAD - HD, GROUP), BF16),
            pltpu.VMEM((GROUP, GROUP), BF16),
            pltpu.VMEM((GROUP, TILE), F32),
            pltpu.VMEM((ROWS, ROWS), BF16),
            pltpu.SemaphoreType.DMA((6,)),
            pltpu.SemaphoreType.DMA((4,)),
            pltpu.SemaphoreType.DMA((4, 2)),
            pltpu.SemaphoreType.DMA((4,)),
            pltpu.SemaphoreType.DMA((4,)),
            pltpu.SemaphoreType.DMA((3,)),
            pltpu.SemaphoreType.DMA((3, 2)),
            pltpu.SemaphoreType.DMA((3,)),
            pltpu.SemaphoreType.DMA((3,)),
        ],
        compiler_params=pltpu.CompilerParams(collective_id=0, has_side_effects=True),
    )(queries, key_states, value_states, out_grads, order, segment_ids)
    return pl.pallas_call(
        last_kernel,
        out_shape=(out, out, out),
        in_specs=[vmem] * 4,
        out_specs=(vmem, vmem, vmem),
    )(*parts, order)


def solution(mesh):
    rows = P(("dp", "seq"), None)
    return jax.shard_map(
        on_device,
        mesh=mesh,
        in_specs=(rows, rows, rows, rows, P(("dp", "seq")), P("dp", None)),
        out_specs=(rows, rows, rows),
        check_vma=False,
    )
```

time: 89.7 us -> 80.8 us (0.901)
  Pallas kernels: 85 us -> 80.1 us
  local copies, waits for them, and re-layouts: 3.58 us -> 0 us
    pallas_call x1 -> x2, Pallas kernels: 85 us -> 80.1 us  [the longest x1 77.8 us: on_device(): pl.pallas_call(kernel, out_shape=(out, out, raw), in_specs=[anywhere] * 6...]
    unnamed x7 -> x0, local copies, waits for them, and re-layouts: 3.58 us -> none
where the time goes in v2:
time: 80.8 us; the launch traced here: 80.7 us
  Pallas kernels  80.1 us (99%)
    pallas_call x1, Pallas kernels, on_device(): pl.pallas_call(kernel, out_shape=(out, out, raw), in_specs=[anywhere] * 6...  77.8 us
    pallas_call x1, Pallas kernels, on_device(): pl.pallas_call(last_kernel, out_shape=(out, out, out), in_specs=[vmem] *...  2.28 us

profile of v2, /device:TPU:1, one launch (start us, length us, event | category | flops | bytes accessed | tf_op | source)
XLA Modules:
  0.0 80.7 jit_solution(10258295273652710188)
XLA Ops:
  0.6 77.8 %shard_map.85 = (bf16[128,1280]{1,0:T(8,128)(2,1)}, bf16[128,1280]{1,0:T(8,128)(2,1)}, bf16[2,16,8,640]{3,2,1,0:T(8,128)(2,1)}) custom-call(bf16[128,1280]{1,0:T(8,128)(2,1)} %q_hbm.1, bf16[128,1280]{1,0:T(8,128)(2,1)} %k_hbm.1, bf16[128,1280]{1,0:T(8,128)(2,1)} %v_hbm.1, bf16[128,1280]{1,0:T(8,128)(2,1)} %g_hbm.1, s32[1,128]{1,0:T(1,128)} %bitcast.1, ...), custom_call_target="tpu_custom_call" | custom-call | tf_op jit(solution)/shard_map/pallas_call | solution.py:447
  78.4 2.3 %shard_map.86 = (bf16[128,1280]{1,0:T(8,128)(2,1)}, bf16[128,1280]{1,0:T(8,128)(2,1)}, bf16[128,1280]{1,0:T(8,128)(2,1)}) custom-call(bf16[128,1280]{1,0:T(8,128)(2,1)} %get-tuple-element.6.gv_ref, bf16[128,1280]{1,0:T(8,128)(2,1)} %get-tuple-element.7.gq_ref, bf16[2,16,8,640]{3,2,1,0:T(8,128)(2,1)} %get-tuple-element.8.raw_ref, s32[1,128]{1,0:T(1,128)} %bitcast.2), custom_call_target="tpu_custom_call" | custom-call | tf_op jit(solution)/shard_map/pallas_call | solution.py:482

commit v3 on v2

v3 whole, which is shorter than its diff:
```python
import functools
import math

import jax
import jax.numpy as jnp
from jax import lax
from jax.experimental import pallas as pl
from jax.experimental.pallas import tpu as pltpu
from jax.sharding import PartitionSpec as P

HD = 80
ROWS = 128
WIDTH = 1280
HALF = 640
SEQ = 16
GROUP = 2048
PAD = 128
MESH = pl.DeviceIdType.MESH
BIG = 1e30
INV_ROOT = 1.0 / math.sqrt(HD)
LOG2E_ROOT = INV_ROOT * math.log2(math.e)
TILE = 256
LOW, HIGH = 6, 10
BANDS = ((0, 3, 0, 5), (3, 5, 0, 8), (5, 8, 3, 8))
K, Q, G, V = 0, 1, 2, 3
GV, GQ, GK = 0, 1, 2
FAR_FIRST = sorted(range(16), key=lambda k: -(k % 2 + (0, 1, 2, 1)[k // 2 % 4]))
BF16 = jnp.bfloat16
F32 = jnp.float32


def dot_nn(a, b):
    return lax.dot_general(a, b, (((1,), (0,)), ((), ())), preferred_element_type=F32)


def dot_nt(a, b):
    return lax.dot_general(a, b, (((1,), (1,)), ((), ())), preferred_element_type=F32)


def identity(n):
    return (
        lax.broadcasted_iota(jnp.int32, (n, n), 0) == lax.broadcasted_iota(jnp.int32, (n, n), 1)
    ).astype(F32).astype(BF16)


def scope(name):
    return jax.named_scope(name)


def onehot_of(order_row):
    return (
        lax.broadcasted_iota(jnp.int32, (ROWS, ROWS), 0)
        == jnp.broadcast_to(order_row, (ROWS, ROWS))
    ).astype(F32).astype(BF16)


def kernel(
    q_hbm, k_hbm, v_hbm, g_hbm, order_hbm, seg_hbm,
    gv_ref, gq_ref, raw_ref, order_t,
    held, order_ref, seg_ref, eye_ref,
    sendz, recvz, send1, recv1, send2, recv2, keys_t,
    send3, recv3, send4, recv4, grad_k, send5, recv5, send6,
    rows_k, rows_v, extra, probs, score,
    load, s0, r0, s1, r1, s2, r2, s3, r3, s4, r4, s5, r5, s6, r6,
):
    dp = lax.axis_index("dp")
    seq = lax.axis_index("seq")
    y_lo = lax.div(seq, 8)
    z = lax.rem(seq, 8)
    core = lax.rem(dp, 2)
    x = lax.rem(lax.div(dp, 2), 4)
    y_hi = lax.div(dp, 8)
    other = 1 - y_lo

    def near(k):
        pc = lax.rem(core + k // 8, 2)
        px = lax.rem(x + k // 2 % 4, 4)
        return lax.rem(y_hi + k % 2, 2) * 8 + px * 2 + pc

    def column(k):
        return lax.rem(z + k, 8)

    def head_rows(k):
        return pl.ds(pl.multiple_of(k * HD, 16), HD)

    def arrive(ref, sem):
        pltpu.make_async_copy(ref, ref, sem).wait()

    barrier = pltpu.get_barrier_semaphore()

    def greet(device):
        pl.semaphore_signal(barrier, inc=1, device_id=device, device_id_type=MESH)

    loads = [
        pltpu.make_async_copy(src, dst, load.at[i])
        for i, (src, dst) in enumerate(
            [(order_hbm, order_ref)]
            + [(ref, held.at[t]) for t, ref in enumerate((k_hbm, q_hbm, g_hbm, v_hbm))]
            + [(seg_hbm, seg_ref)]
        )
    ]
    for copy in loads:
        copy.start()
    with scope("A_greet"):
        for k in (4, 3, 5, 2, 6, 1, 7):
            greet((dp, y_lo * 8 + column(k)))
        for k in FAR_FIRST:
            pd = near(k)
            greet((pd, other * 8 + z))
            if k:
                greet((pd, seq))

    eye_ref[...] = identity(ROWS)

    def to_rows(src, dst):
        for c in range(5):
            part = dot_nt(eye_ref[...], src[c * 128:(c + 1) * 128])
            dst[:, :, c * 128:(c + 1) * 128] = part.reshape(16, 8, 128).astype(BF16)

    def to_columns(src, dst):
        rows = src[...].astype(F32).reshape(ROWS, HALF).astype(BF16)
        for c in range(5):
            part = dot_nt(eye_ref[...], rows[:, c * 128:(c + 1) * 128])
            dst[c * 128:(c + 1) * 128] = part.astype(BF16)

    def plane_send(src, dst, half, send_sem, recv_sem):
        for k in FAR_FIRST:
            pd = near(k)

            def remote(pd=pd):
                pltpu.make_async_remote_copy(
                    src_ref=src.at[pd],
                    dst_ref=dst.at[y_lo, dp],
                    send_sem=send_sem,
                    recv_sem=recv_sem.at[y_lo],
                    device_id=(pd, half * 8 + z),
                    device_id_type=MESH,
                ).start()

            def local():
                pltpu.make_async_copy(
                    src.at[dp], dst.at[y_lo, dp], recv_sem.at[y_lo]
                ).start()

            if k:
                remote()
            else:
                pl.when(half != y_lo)(remote)
                pl.when(half == y_lo)(local)

    def column_send(src, dst, send_sem, recv_sem):
        for k in (4, 3, 5, 2, 6, 1, 7):
            pz = column(k)
            pltpu.make_async_remote_copy(
                src_ref=src.at[head_rows(pz)],
                dst_ref=dst,
                send_sem=send_sem,
                recv_sem=recv_sem,
                device_id=(dp, y_lo * 8 + pz),
                device_id_type=MESH,
            ).start()
        pltpu.make_async_copy(src.at[head_rows(z)], dst, recv_sem).start()

    def permuted(t, half, onehot):
        return dot_nn(onehot, held[t, :, half * HALF:(half + 1) * HALF])

    def permute(t, onehot):
        loads[1 + t].wait()
        for half in range(2):
            send1[t, half] = permuted(t, half, onehot).reshape(16, 8, HALF).astype(BF16)

    def start1(t):
        for half in (other, y_lo):
            plane_send(send1.at[t, half], recv1.at[t], half, s1.at[t], r1.at[t])

    def start2(t):
        for half in (other, y_lo):
            with scope("wait1"):
                arrive(recv1.at[t, half], r1.at[t, half])
            to_columns(recv1.at[t, half], send2.at[t, half])
            column_send(send2.at[t, half], recv2.at[t, half * 8 + z], s2.at[t], r2.at[t])

    def arrived2(t):
        with scope("wait2"):
            arrive(recv2.at[t], r2.at[t])

    def block(t, s):
        if t == K:
            return keys_t[s // 8, s % 8 * HD:(s % 8 + 1) * HD]
        return recv2[t, s]

    def wide(t, first, last):
        return jnp.concatenate([block(t, s) for s in range(first, last)], axis=1)

    with scope("A_permK"):
        loads[0].wait()
        onehot_t = onehot_of(order_ref[...])
        order_t[...] = onehot_t
        onehot = dot_nt(eye_ref[...], onehot_t).astype(BF16)
        loads[1 + K].wait()
        for half in range(2):
            rows = permuted(K, half, onehot).astype(BF16)
            for c in range(5):
                part = dot_nt(eye_ref[...], rows[:, c * 128:(c + 1) * 128])
                sendz[half, c * 128:(c + 1) * 128] = part.astype(BF16)
    with scope("A_permQ"):
        permute(Q, onehot)
    with scope("A_barrier"):
        pl.semaphore_wait(barrier, 38)
    with scope("A_sendz"):
        for half in (other, y_lo):
            column_send(sendz.at[half], recvz.at[half, head_rows(z)], s0, r0.at[half])
    with scope("A_start1Q"):
        start1(Q)
    with scope("A_permGV"):
        permute(G, onehot)
    with scope("B_start1G"):
        start1(G)
    with scope("A_permGV"):
        permute(V, onehot)
        loads[5].wait()
        index = lax.broadcasted_iota(jnp.int32, (PAD - HD, GROUP), 0)
        seg = jnp.broadcast_to(seg_ref[...].astype(F32), (PAD - HD, GROUP))
        first, second = index == 0, index == 1
        extra[0] = jnp.where(first, seg, jnp.where(second, 1.0 - seg, 0.0)).astype(BF16)
        extra[1] = jnp.where(
            first, -BIG * (1.0 - seg), jnp.where(second, -BIG * seg, 0.0)
        ).astype(BF16)

    def keys_on(half):
        with scope("wait0"):
            arrive(recvz.at[half], r0.at[half])
        to_rows(recvz.at[half], send1.at[K, half])
        plane_send(send1.at[K, half], recv1.at[K], half, s1.at[K], r1.at[K])

    with scope("B_start2Q"):
        start2(Q)
    with scope("B_keysA"):
        keys_on(other)
    with scope("B_keysB"):
        keys_on(y_lo)
    with scope("B_start1V"):
        start1(V)
    with scope("B_start2G"):
        start2(G)

    with scope("B_keysin"):
        for half in range(2):
            with scope("waitK"):
                arrive(recv1.at[K, half], r1.at[K, half])
            to_columns(recv1.at[K, half], keys_t.at[half])
        for s in range(SEQ):
            full = jnp.concatenate([block(K, s), extra[0, :, s * ROWS:(s + 1) * ROWS]], axis=0)
            rows_k[s * ROWS:(s + 1) * ROWS] = dot_nt(eye_ref[...], full).astype(BF16)
    arrived2(Q)

    def pair_of(t, qt):
        return jnp.concatenate([recv2[t, 2 * qt], recv2[t, 2 * qt + 1]], axis=1)

    for q_first, q_last, k_first, k_last in BANDS:

        def soft_tile(qt, c, k_first=k_first, k_last=k_last):
            lanes = pl.ds(pl.multiple_of(qt * TILE, TILE), TILE)
            q_t = jnp.concatenate([pair_of(Q, qt), extra[1, :, lanes]], axis=0)
            top = jnp.full((8, TILE), -jnp.inf, F32)
            for kt in range(k_first, k_last):
                part = dot_nn(rows_k[kt * TILE:(kt + 1) * TILE], q_t)
                score[kt * TILE:(kt + 1) * TILE] = part
                top = jnp.maximum(top, jnp.max(part.reshape(TILE // 8, 8, TILE), axis=0))
            top = jnp.max(top, axis=0, keepdims=True) * LOG2E_ROOT
            total = jnp.zeros((8, TILE), F32)
            for kt in range(k_first, k_last):
                part = jnp.exp2(score[kt * TILE:(kt + 1) * TILE] * LOG2E_ROOT - top)
                score[kt * TILE:(kt + 1) * TILE] = part
                total = total + jnp.sum(part.reshape(TILE // 8, 8, TILE), axis=0)
            scale = 1.0 / jnp.sum(total, axis=0, keepdims=True)
            for kt in range(k_first, k_last):
                probs[kt * TILE:(kt + 1) * TILE, lanes] = (
                    score[kt * TILE:(kt + 1) * TILE] * scale
                ).astype(BF16)
            return c

        with scope("C_soft"):
            lax.fori_loop(q_first, q_last, soft_tile, 0)
        if q_first == 0:
            with scope("B_start2V"):
                start2(V)

    def start3(t, half, pz):
        s = half * 8 + pz
        dst = recv3.at[t, half, head_rows(z)]

        @pl.when(pz != z)
        def _():
            pltpu.make_async_remote_copy(
                src_ref=send3.at[t, s],
                dst_ref=dst,
                send_sem=s3.at[t],
                recv_sem=r3.at[t, half],
                device_id=(dp, y_lo * 8 + pz),
                device_id_type=MESH,
            ).start()

        @pl.when(pz == z)
        def _():
            pltpu.make_async_copy(send3.at[t, s], dst, r3.at[t, half]).start()

    def key_side(source, band, done):
        k_first, k_last, q_first, q_last = band
        left = wide(source, 2 * q_first, 2 * q_last)
        for kt in range(k_first, k_last):
            done(
                kt,
                dot_nt(left, probs[kt * TILE:(kt + 1) * TILE, q_first * TILE:q_last * TILE]),
            )

    arrived2(G)
    with scope("C_gv"):

        def gv_done(kt, part):
            part = part.astype(BF16)
            send3[GV, 2 * kt] = part[:, :ROWS]
            send3[GV, 2 * kt + 1] = part[:, ROWS:]

        for band in BANDS:
            key_side(G, band, gv_done)
    with scope("C_start3"):
        for half in range(2):

            def one(k, c, half=half):
                start3(GV, half, column(k))
                return c

            lax.fori_loop(4, 12, one, 0)

    arrived2(V)
    tail = (lax.broadcasted_iota(jnp.int32, (PAD - HD, ROWS), 0) < 3).astype(F32).astype(BF16)
    for s in range(SEQ):
        full = jnp.concatenate([recv2[V, s], tail], axis=0)
        rows_v[s * ROWS:(s + 1) * ROWS] = dot_nt(eye_ref[...], full).astype(BF16)

    def grad_tile(qt, k_first, k_last):
        lanes = pl.ds(pl.multiple_of(qt * TILE, TILE), TILE)
        g_t = pair_of(G, qt)
        keys = slice(k_first * TILE, k_last * TILE)
        attended = dot_nn(wide(V, 2 * k_first, 2 * k_last), probs[keys, lanes])
        delta = -jnp.sum(g_t.astype(F32) * attended, axis=0, keepdims=True)
        high = delta.astype(BF16).astype(F32)
        middle = (delta - high).astype(BF16).astype(F32)
        low = delta - high - middle
        index = lax.broadcasted_iota(jnp.int32, (PAD - HD, TILE), 0)
        more = jnp.where(
            index == 0, high, jnp.where(index == 1, middle, jnp.where(index == 2, low, 0.0))
        ).astype(BF16)
        g_t = jnp.concatenate([g_t, more], axis=0)
        for kt in range(k_first, k_last):
            part = dot_nn(rows_v[kt * TILE:(kt + 1) * TILE], g_t)
            part = part * probs[kt * TILE:(kt + 1) * TILE, lanes].astype(F32)
            probs[kt * TILE:(kt + 1) * TILE, lanes] = part.astype(BF16)
        grad = dot_nn(wide(K, 2 * k_first, 2 * k_last), probs[keys, lanes]) * INV_ROOT
        grad = grad.astype(BF16)
        send3[GQ, 2 * qt] = grad[:, :ROWS]
        send3[GQ, 2 * qt + 1] = grad[:, ROWS:]

    def grad_step(i, c):
        pair = lax.rem(lax.div(z, 2) + 1 + lax.div(i, 2), 4)
        half = lax.rem(i, 2)
        qt = pair + 4 * half
        for q_first, q_last, k_first, k_last in BANDS:

            @pl.when(jnp.logical_and(qt >= q_first, qt < q_last))
            def _(k_first=k_first, k_last=k_last):
                grad_tile(qt, k_first, k_last)

        for j in range(2):
            start3(GQ, half, 2 * pair + j)
        return c

    with scope("D_grad"):
        lax.fori_loop(0, 8, grad_step, 0)

    with scope("D_gk"):

        def gk_done(kt, part):
            part = (part * INV_ROOT).astype(BF16)
            for j in range(2):
                s = 2 * kt + j
                grad_k[s // 8, s % 8 * HD:(s % 8 + 1) * HD] = part[:, j * ROWS:(j + 1) * ROWS]
            if kt % 4 == 3:
                half = kt // 4
                to_rows(grad_k.at[half], send5.at[half])
                plane_send(send5.at[half], recv5, half, s5, r5)

        for band in BANDS:
            key_side(Q, band, gk_done)

    def start4(t):
        for half in (y_lo, other):
            with scope("wait3"):
                arrive(recv3.at[t, half], r3.at[t, half])
            to_rows(recv3.at[t, half], send4.at[t, half])
            plane_send(send4.at[t, half], recv4.at[t], half, s4.at[t], r4.at[t])

    def finish(t, ref):
        for half in range(2):
            with scope("wait4"):
                arrive(recv4.at[t, half], r4.at[t, half])
            rows = recv4[t, half].astype(F32).reshape(ROWS, HALF).astype(BF16)
            held[t, :, half * HALF:(half + 1) * HALF] = dot_nn(order_t[...], rows).astype(BF16)
        pltpu.make_async_copy(held.at[t], ref, load.at[t]).start()

    with scope("E_start4V"):
        start4(GV)
    with scope("E_gk_on"):
        for half in (y_lo, other):
            with scope("wait5"):
                arrive(recv5.at[half], r5.at[half])
            to_columns(recv5.at[half], send6.at[half])
            column_send(send6.at[half], raw_ref.at[head_rows(half * 8 + z)], s6, r6)
    with scope("E_start4Q"):
        start4(GQ)
    with scope("E_finV"):
        finish(GV, gv_ref)
    with scope("E_finQ"):
        finish(GQ, gq_ref)

    with scope("E_sent"):
        def left(ref, sem):
            pltpu.make_async_copy(ref, ref, sem).wait()

        def plane_left(ref, sem):
            left(ref.at[0], sem)
            left(ref.at[1, pl.ds(0, 15)], sem)

        for t in range(4):
            plane_left(send1.at[t], s1.at[t])
        column_all = recv2.at[Q, pl.ds(0, 14)]
        left(column_all, s0)
        for t in (Q, G, V):
            left(column_all, s2.at[t])
        for t in range(2):
            left(column_all, s3.at[t])
            plane_left(send4.at[t], s4.at[t])
        plane_left(send5, s5)
        left(column_all, s6)
    with scope("E_last"):
        for t, ref in ((GV, gv_ref), (GQ, gq_ref)):
            pltpu.make_async_copy(held.at[t], ref, load.at[t]).wait()
        arrive(raw_ref, r6)


def last_kernel(gv_ref, gq_ref, raw_ref, order_t, gq_out, gk_out, gv_out):
    gk_out[...] = dot_nt(order_t[...], raw_ref[...]).astype(BF16)
    gv_out[...] = gv_ref[...]
    gq_out[...] = gq_ref[...]


def on_device(queries, key_states, value_states, out_grads, row_order, segment_ids):
    out = jax.ShapeDtypeStruct((ROWS, WIDTH), BF16)
    raw = jax.ShapeDtypeStruct((WIDTH, ROWS), BF16)
    vmem = pl.BlockSpec(memory_space=pltpu.VMEM)
    anywhere = pl.BlockSpec(memory_space=pl.ANY)
    order = row_order[None, :]
    rows_form = (2, 16, 8, HALF)
    columns_form = (2, HALF, ROWS)
    dma = pltpu.SemaphoreType.DMA
    inputs = (queries, key_states, value_states, out_grads, order, segment_ids)
    parts = pl.pallas_call(
        kernel,
        out_shape=(out, out, raw, jax.ShapeDtypeStruct((ROWS, ROWS), BF16)),
        in_specs=[pl.BlockSpec(memory_space=pltpu.HBM)] * 6,
        out_specs=(anywhere, anywhere, anywhere, vmem),
        scratch_shapes=[
            pltpu.VMEM((4, ROWS, WIDTH), BF16),
            pltpu.VMEM((1, ROWS), jnp.int32),
            pltpu.VMEM((1, GROUP), jnp.int32),
            pltpu.VMEM((ROWS, ROWS), BF16),
            pltpu.VMEM(columns_form, BF16),
            pltpu.VMEM(columns_form, BF16),
            pltpu.VMEM((4, *rows_form), BF16),
            pltpu.VMEM((4, *rows_form), BF16),
            pltpu.VMEM((4, *columns_form), BF16),
            pltpu.VMEM((4, SEQ, HD, ROWS), BF16),
            pltpu.VMEM(columns_form, BF16),
            pltpu.VMEM((2, SEQ, HD, ROWS), BF16),
            pltpu.VMEM((2, *columns_form), BF16),
            pltpu.VMEM((2, *rows_form), BF16),
            pltpu.VMEM((2, *rows_form), BF16),
            pltpu.VMEM(columns_form, BF16),
            pltpu.VMEM(rows_form, BF16),
            pltpu.VMEM(rows_form, BF16),
            pltpu.VMEM(columns_form, BF16),
            pltpu.VMEM((GROUP, PAD), BF16),
            pltpu.VMEM((GROUP, PAD), BF16),
            pltpu.VMEM((2, PAD - HD, GROUP), BF16),
            pltpu.VMEM((GROUP, GROUP), BF16),
            pltpu.VMEM((GROUP, TILE), F32),
            dma((6,)),
            dma, dma((2,)),
            dma((4,)), dma((4, 2)),
            dma((4,)), dma((4,)),
            dma((2,)), dma((2, 2)),
            dma((2,)), dma((2, 2)),
            dma, dma((2,)),
            dma, dma,
        ],
        compiler_params=pltpu.CompilerParams(
            collective_id=0, has_side_effects=True, vmem_limit_bytes=40 << 20
        ),
    )(*(pltpu.with_memory_space_constraint(a, pltpu.HBM) for a in inputs))
    return pl.pallas_call(
        last_kernel,
        out_shape=(out, out, out),
        in_specs=[vmem] * 4,
        out_specs=(vmem, vmem, vmem),
        compiler_params=pltpu.CompilerParams(vmem_limit_bytes=8 << 20),
    )(*parts)


def solution(mesh):
    rows = P(("dp", "seq"), None)
    return jax.shard_map(
        on_device,
        mesh=mesh,
        in_specs=(rows, rows, rows, rows, P(("dp", "seq")), P("dp", None)),
        out_specs=(rows, rows, rows),
        check_vma=False,
    )
```

time: 80.8 us -> 70.9 us (0.88)
  Pallas kernels: 80.1 us -> 70.1 us
    pallas_call x1, Pallas kernels: 77.8 us -> 69 us  [on_device(): pl.pallas_call(kernel, out_shape=(out, out, raw, jax.ShapeDtypeStruct((RO...]
    pallas_call x1, Pallas kernels: 2.28 us -> 1.13 us  [on_device(): pl.pallas_call(last_kernel, out_shape=(out, out, out), in_specs=[vmem] *...]
where the time goes in v3:
time: 70.9 us; the launch traced here: 70.8 us
  Pallas kernels  70.1 us (99%)
    pallas_call x1, Pallas kernels, on_device(): pl.pallas_call(kernel, out_shape=(out, out, raw, jax.ShapeDtypeStruct((RO...  69 us

profile of v3, /device:TPU:1, one launch (start us, length us, event | category | flops | bytes accessed | tf_op | source)
XLA Modules:
  0.0 70.8 jit_solution(867311556276415365)
XLA Ops:
  0.6 69.0 %shard_map.85 = (bf16[128,1280]{1,0:T(8,128)(2,1)S(1)}, bf16[128,1280]{1,0:T(8,128)(2,1)S(1)}, bf16[1280,128]{1,0:T(8,128)(2,1)S(1)}, bf16[128,128]{1,0:T(8,128)(2,1)S(1)}) custom-call(bf16[128,1280]{1,0:T(8,128)(2,1)} %q_hbm.1, bf16[128,1280]{1,0:T(8,128)(2,1)} %k_hbm.1, bf16[128,1280]{1,0:T(8,128)(2,1)} %v_hbm.1, bf16[128,1280]{1,0:T(8,128)(2,1)} %g_hbm.1, ...), custom_call_target="tpu_custom_call" | custom-call | tf_op jit(solution)/shard_map/pallas_call | solution.py:468
  69.7 1.1 %shard_map.86 = (bf16[128,1280]{1,0:T(8,128)(2,1)}, bf16[128,1280]{1,0:T(8,128)(2,1)}, bf16[128,1280]{1,0:T(8,128)(2,1)}) custom-call(bf16[128,1280]{1,0:T(8,128)(2,1)S(1)} %get-tuple-element.7.gv_ref, bf16[128,1280]{1,0:T(8,128)(2,1)S(1)} %get-tuple-element.8.gq_ref, bf16[1280,128]{1,0:T(8,128)(2,1)S(1)} %get-tuple-element.9.raw_ref, ...), custom_call_target="tpu_custom_call" | custom-call | tf_op jit(solution)/shard_map/pallas_call | solution.py:511

commit v4 on v3

--- a/solution.py
+++ b/solution.py
@@ -23,7 +23,7 @@
 LOW, HIGH = 6, 10
 BANDS = ((0, 3, 0, 5), (3, 5, 0, 8), (5, 8, 3, 8))
 K, Q, G, V = 0, 1, 2, 3
-GV, GQ, GK = 0, 1, 2
+GV, GK, GQ = 0, 1, 2
 FAR_FIRST = sorted(range(16), key=lambda k: -(k % 2 + (0, 1, 2, 1)[k // 2 % 4]))
 BF16 = jnp.bfloat16
 F32 = jnp.float32
@@ -56,10 +56,10 @@
 
 def kernel(
     q_hbm, k_hbm, v_hbm, g_hbm, order_hbm, seg_hbm,
-    gv_ref, gq_ref, raw_ref, order_t,
+    gv_ref, gk_ref, raw_ref, order_t,
     held, order_ref, seg_ref, eye_ref,
     sendz, recvz, send1, recv1, send2, recv2, keys_t,
-    send3, recv3, send4, recv4, grad_k, send5, recv5, send6,
+    send3, recv3, send4, recv4, grad_q, send5, recv5, send6,
     rows_k, rows_v, extra, probs, score,
     load, s0, r0, s1, r1, s2, r2, s3, r3, s4, r4, s5, r5, s6, r6,
 ):
@@ -257,32 +257,41 @@
     def pair_of(t, qt):
         return jnp.concatenate([recv2[t, 2 * qt], recv2[t, 2 * qt + 1]], axis=1)
 
-    for q_first, q_last, k_first, k_last in BANDS:
-
-        def soft_tile(qt, c, k_first=k_first, k_last=k_last):
-            lanes = pl.ds(pl.multiple_of(qt * TILE, TILE), TILE)
-            q_t = jnp.concatenate([pair_of(Q, qt), extra[1, :, lanes]], axis=0)
-            top = jnp.full((8, TILE), -jnp.inf, F32)
-            for kt in range(k_first, k_last):
-                part = dot_nn(rows_k[kt * TILE:(kt + 1) * TILE], q_t)
-                score[kt * TILE:(kt + 1) * TILE] = part
-                top = jnp.maximum(top, jnp.max(part.reshape(TILE // 8, 8, TILE), axis=0))
-            top = jnp.max(top, axis=0, keepdims=True) * LOG2E_ROOT
-            total = jnp.zeros((8, TILE), F32)
-            for kt in range(k_first, k_last):
-                part = jnp.exp2(score[kt * TILE:(kt + 1) * TILE] * LOG2E_ROOT - top)
-                score[kt * TILE:(kt + 1) * TILE] = part
-                total = total + jnp.sum(part.reshape(TILE // 8, 8, TILE), axis=0)
-            scale = 1.0 / jnp.sum(total, axis=0, keepdims=True)
-            for kt in range(k_first, k_last):
-                probs[kt * TILE:(kt + 1) * TILE, lanes] = (
-                    score[kt * TILE:(kt + 1) * TILE] * scale
-                ).astype(BF16)
-            return c
-
+    def band_of(tile):
+        return next(band[2:] for band in BANDS if band[0] <= tile < band[1])
+
+    def soft_tiles(tiles):
+        tops, totals, sides, scales = {}, {}, {}, {}
+        steps = [
+            (n, qt, slice(kt * TILE, (kt + 1) * TILE))
+            for kt in range(8)
+            for n, qt in enumerate(tiles)
+            if band_of(qt)[0] <= kt < band_of(qt)[1]
+        ]
+        for qt in tiles:
+            lanes = slice(qt * TILE, (qt + 1) * TILE)
+            sides[qt] = jnp.concatenate([pair_of(Q, qt), extra[1, :, lanes]], axis=0)
+            tops[qt] = jnp.full((8, TILE), -jnp.inf, F32)
+            totals[qt] = jnp.zeros((8, TILE), F32)
+        for n, qt, rows in steps:
+            part = dot_nn(rows_k[rows], sides[qt])
+            score[n, rows] = part
+            tops[qt] = jnp.maximum(tops[qt], jnp.max(part.reshape(TILE // 8, 8, TILE), axis=0))
+        for qt in tiles:
+            tops[qt] = jnp.max(tops[qt], axis=0, keepdims=True) * LOG2E_ROOT
+        for n, qt, rows in steps:
+            part = jnp.exp2(score[n, rows] * LOG2E_ROOT - tops[qt])
+            score[n, rows] = part
+            totals[qt] = totals[qt] + jnp.sum(part.reshape(TILE // 8, 8, TILE), axis=0)
+        for qt in tiles:
+            scales[qt] = 1.0 / jnp.sum(totals[qt], axis=0, keepdims=True)
+        for n, qt, rows in steps:
+            probs[rows, qt * TILE:(qt + 1) * TILE] = (score[n, rows] * scales[qt]).astype(BF16)
+
+    for pair in range(4):
         with scope("C_soft"):
-            lax.fori_loop(q_first, q_last, soft_tile, 0)
-        if q_first == 0:
+            soft_tiles((pair, pair + 4))
+        if pair == 0:
             with scope("B_start2V"):
                 start2(V)
 
@@ -324,14 +333,16 @@
 
         for band in BANDS:
             key_side(G, band, gv_done)
+    def start3_half(t, half):
+        def one(k, c):
+            start3(t, half, column(k))
+            return c
+
+        lax.fori_loop(4, 12, one, 0)
+
     with scope("C_start3"):
-        for half in range(2):
-
-            def one(k, c, half=half):
-                start3(GV, half, column(k))
-                return c
-
-            lax.fori_loop(4, 12, one, 0)
+        start3_half(GV, 0)
+        start3_half(GV, 1)
 
     arrived2(V)
     tail = (lax.broadcasted_iota(jnp.int32, (PAD - HD, ROWS), 0) < 3).astype(F32).astype(BF16)
@@ -339,67 +350,76 @@
         full = jnp.concatenate([recv2[V, s], tail], axis=0)
         rows_v[s * ROWS:(s + 1) * ROWS] = dot_nt(eye_ref[...], full).astype(BF16)
 
-    def grad_tile(qt, k_first, k_last):
-        lanes = pl.ds(pl.multiple_of(qt * TILE, TILE), TILE)
-        g_t = pair_of(G, qt)
-        keys = slice(k_first * TILE, k_last * TILE)
-        attended = dot_nn(wide(V, 2 * k_first, 2 * k_last), probs[keys, lanes])
-        delta = -jnp.sum(g_t.astype(F32) * attended, axis=0, keepdims=True)
-        high = delta.astype(BF16).astype(F32)
-        middle = (delta - high).astype(BF16).astype(F32)
-        low = delta - high - middle
-        index = lax.broadcasted_iota(jnp.int32, (PAD - HD, TILE), 0)
-        more = jnp.where(
-            index == 0, high, jnp.where(index == 1, middle, jnp.where(index == 2, low, 0.0))
-        ).astype(BF16)
-        g_t = jnp.concatenate([g_t, more], axis=0)
-        for kt in range(k_first, k_last):
-            part = dot_nn(rows_v[kt * TILE:(kt + 1) * TILE], g_t)
-            part = part * probs[kt * TILE:(kt + 1) * TILE, lanes].astype(F32)
-            probs[kt * TILE:(kt + 1) * TILE, lanes] = part.astype(BF16)
-        grad = dot_nn(wide(K, 2 * k_first, 2 * k_last), probs[keys, lanes]) * INV_ROOT
-        grad = grad.astype(BF16)
-        send3[GQ, 2 * qt] = grad[:, :ROWS]
-        send3[GQ, 2 * qt + 1] = grad[:, ROWS:]
-
-    def grad_step(i, c):
-        pair = lax.rem(lax.div(z, 2) + 1 + lax.div(i, 2), 4)
-        half = lax.rem(i, 2)
-        qt = pair + 4 * half
-        for q_first, q_last, k_first, k_last in BANDS:
-
-            @pl.when(jnp.logical_and(qt >= q_first, qt < q_last))
-            def _(k_first=k_first, k_last=k_last):
-                grad_tile(qt, k_first, k_last)
-
-        for j in range(2):
-            start3(GQ, half, 2 * pair + j)
-        return c
-
-    with scope("D_grad"):
-        lax.fori_loop(0, 8, grad_step, 0)
-
-    with scope("D_gk"):
-
-        def gk_done(kt, part):
+    def grad_pair(pair):
+        tiles = []
+        for qt in (pair, pair + 4):
+            k_first, k_last = band_of(qt)
+            lanes = slice(qt * TILE, (qt + 1) * TILE)
+            tiles.append((qt, k_first, k_last, lanes, slice(k_first * TILE, k_last * TILE)))
+        sides = []
+        for qt, k_first, k_last, lanes, keys in tiles:
+            g_t = pair_of(G, qt)
+            attended = dot_nn(wide(V, 2 * k_first, 2 * k_last), probs[keys, lanes])
+            delta = -jnp.sum(g_t.astype(F32) * attended, axis=0, keepdims=True)
+            high = delta.astype(BF16).astype(F32)
+            middle = (delta - high).astype(BF16).astype(F32)
+            low = delta - high - middle
+            index = lax.broadcasted_iota(jnp.int32, (PAD - HD, TILE), 0)
+            more = jnp.where(
+                index == 0, high, jnp.where(index == 1, middle, jnp.where(index == 2, low, 0.0))
+            ).astype(BF16)
+            sides.append(jnp.concatenate([g_t, more], axis=0))
+        for kt in range(8):
+            for (qt, k_first, k_last, lanes, keys), g_t in zip(tiles, sides):
+                if k_first <= kt < k_last:
+                    rows = slice(kt * TILE, (kt + 1) * TILE)
+                    part = dot_nn(rows_v[rows], g_t) * probs[rows, lanes].astype(F32)
+                    probs[rows, lanes] = part.astype(BF16)
+
+    for pair in range(4):
+        with scope("D_grad"):
+            grad_pair(pair)
+
+    def start4(t, half):
+        with scope("wait3"):
+            arrive(recv3.at[t, half], r3.at[t, half])
+        to_rows(recv3.at[t, half], send4.at[t, half])
+        plane_send(send4.at[t, half], recv4.at[t], half, s4.at[t], r4.at[t])
+
+    def gk_half(half):
+        for kt in range(4 * half, 4 * half + 4):
+            q_first, q_last = band_of(kt)
+            part = dot_nt(
+                wide(Q, 2 * q_first, 2 * q_last),
+                probs[kt * TILE:(kt + 1) * TILE, q_first * TILE:q_last * TILE],
+            )
             part = (part * INV_ROOT).astype(BF16)
-            for j in range(2):
-                s = 2 * kt + j
-                grad_k[s // 8, s % 8 * HD:(s % 8 + 1) * HD] = part[:, j * ROWS:(j + 1) * ROWS]
-            if kt % 4 == 3:
-                half = kt // 4
-                to_rows(grad_k.at[half], send5.at[half])
-                plane_send(send5.at[half], recv5, half, s5, r5)
-
-        for band in BANDS:
-            key_side(Q, band, gk_done)
-
-    def start4(t):
-        for half in (y_lo, other):
-            with scope("wait3"):
-                arrive(recv3.at[t, half], r3.at[t, half])
-            to_rows(recv3.at[t, half], send4.at[t, half])
-            plane_send(send4.at[t, half], recv4.at[t], half, s4.at[t], r4.at[t])
+            send3[GK, 2 * kt] = part[:, :ROWS]
+            send3[GK, 2 * kt + 1] = part[:, ROWS:]
+        start3_half(GK, half)
+
+    with scope("D_gk0"):
+        gk_half(0)
+    for half in range(2):
+        with scope("D_gq"):
+            for qt in range(4 * half, 4 * half + 4):
+                k_first, k_last = band_of(qt)
+                grad = dot_nn(
+                    wide(K, 2 * k_first, 2 * k_last),
+                    probs[k_first * TILE:k_last * TILE, qt * TILE:(qt + 1) * TILE],
+                )
+                grad = (grad * INV_ROOT).astype(BF16)
+                for j in range(2):
+                    p = (2 * qt + j) % 8
+                    grad_q[half, p * HD:(p + 1) * HD] = grad[:, j * ROWS:(j + 1) * ROWS]
+            to_rows(grad_q.at[half], send5.at[half])
+            plane_send(send5.at[half], recv5, half, s5, r5)
+    with scope("D_gk1"):
+        gk_half(1)
+    with scope("E_start4V0"):
+        start4(GV, 0)
+    with scope("E_start4V1"):
+        start4(GV, 1)
 
     def finish(t, ref):
         for half in range(2):
@@ -409,20 +429,19 @@
             held[t, :, half * HALF:(half + 1) * HALF] = dot_nn(order_t[...], rows).astype(BF16)
         pltpu.make_async_copy(held.at[t], ref, load.at[t]).start()
 
-    with scope("E_start4V"):
-        start4(GV)
-    with scope("E_gk_on"):
+    with scope("E_gq_on"):
         for half in (y_lo, other):
             with scope("wait5"):
                 arrive(recv5.at[half], r5.at[half])
             to_columns(recv5.at[half], send6.at[half])
             column_send(send6.at[half], raw_ref.at[head_rows(half * 8 + z)], s6, r6)
-    with scope("E_start4Q"):
-        start4(GQ)
+    with scope("E_start4K"):
+        start4(GK, 0)
+        start4(GK, 1)
     with scope("E_finV"):
         finish(GV, gv_ref)
-    with scope("E_finQ"):
-        finish(GQ, gq_ref)
+    with scope("E_finK"):
+        finish(GK, gk_ref)
 
     with scope("E_sent"):
         def left(ref, sem):
@@ -444,15 +463,15 @@
         plane_left(send5, s5)
         left(column_all, s6)
     with scope("E_last"):
-        for t, ref in ((GV, gv_ref), (GQ, gq_ref)):
+        for t, ref in ((GV, gv_ref), (GK, gk_ref)):
             pltpu.make_async_copy(held.at[t], ref, load.at[t]).wait()
         arrive(raw_ref, r6)
 
 
-def last_kernel(gv_ref, gq_ref, raw_ref, order_t, gq_out, gk_out, gv_out):
-    gk_out[...] = dot_nt(order_t[...], raw_ref[...]).astype(BF16)
+def last_kernel(gv_ref, gk_ref, raw_ref, order_t, gq_out, gk_out, gv_out):
+    gq_out[...] = dot_nt(order_t[...], raw_ref[...]).astype(BF16)
     gv_out[...] = gv_ref[...]
-    gq_out[...] = gq_ref[...]
+    gk_out[...] = gk_ref[...]
 
 
 def on_device(queries, key_states, value_states, out_grads, row_order, segment_ids):
@@ -494,7 +513,7 @@
             pltpu.VMEM((GROUP, PAD), BF16),
             pltpu.VMEM((2, PAD - HD, GROUP), BF16),
             pltpu.VMEM((GROUP, GROUP), BF16),
-            pltpu.VMEM((GROUP, TILE), F32),
+            pltpu.VMEM((2, GROUP, TILE), F32),
             dma((6,)),
             dma, dma((2,)),
             dma((4,)), dma((4, 2)),

time: 70.9 us -> 65.6 us (0.925)
  Pallas kernels: 70.1 us -> 64.9 us
    pallas_call x1, Pallas kernels: 69 us -> 63.8 us  [on_device(): pl.pallas_call(kernel, out_shape=(out, out, raw, jax.ShapeDtypeStruct((RO...]
where the time goes in v4:
time: 65.6 us; the launch traced here: 65.5 us
  Pallas kernels  64.9 us (99%)
    pallas_call x1, Pallas kernels, on_device(): pl.pallas_call(kernel, out_shape=(out, out, raw, jax.ShapeDtypeStruct((RO...  63.8 us

profile of v4, /device:TPU:1, one launch (start us, length us, event | category | flops | bytes accessed | tf_op | source)
XLA Modules:
  0.0 65.5 jit_solution(17716325632838044841)
XLA Ops:
  0.6 63.8 %shard_map.85 = (bf16[128,1280]{1,0:T(8,128)(2,1)S(1)}, bf16[128,1280]{1,0:T(8,128)(2,1)S(1)}, bf16[1280,128]{1,0:T(8,128)(2,1)S(1)}, bf16[128,128]{1,0:T(8,128)(2,1)S(1)}) custom-call(bf16[128,1280]{1,0:T(8,128)(2,1)} %q_hbm.1, bf16[128,1280]{1,0:T(8,128)(2,1)} %k_hbm.1, bf16[128,1280]{1,0:T(8,128)(2,1)} %v_hbm.1, bf16[128,1280]{1,0:T(8,128)(2,1)} %g_hbm.1, ...), custom_call_target="tpu_custom_call" | custom-call | tf_op jit(solution)/shard_map/pallas_call | solution.py:487
  64.4 1.1 %shard_map.86 = (bf16[128,1280]{1,0:T(8,128)(2,1)}, bf16[128,1280]{1,0:T(8,128)(2,1)}, bf16[128,1280]{1,0:T(8,128)(2,1)}) custom-call(bf16[128,1280]{1,0:T(8,128)(2,1)S(1)} %get-tuple-element.7.gv_ref, bf16[128,1280]{1,0:T(8,128)(2,1)S(1)} %get-tuple-element.8.gk_ref, bf16[1280,128]{1,0:T(8,128)(2,1)S(1)} %get-tuple-element.9.raw_ref, ...), custom_call_target="tpu_custom_call" | custom-call | tf_op jit(solution)/shard_map/pallas_call | solution.py:530
